TPU v7x, 256 devices: a whole 4x4x8 slice. The times are simulated.
256 devices in a mesh: group: 16 (over y_hi, z), member: 16 (over y_lo, x, core).
Axes of the slice: x: 4, y: 4 (y_hi: 2, y_lo: 2; y = y_hi * 2 + y_lo), z: 8, core: 2. Of those that a mesh axis runs over, the one named last changes fastest.
Arguments:
- points: float32 [256, 8, 1024], P(('group', 'member')), may hold values from -4 to 4
- inverse_cov: bfloat16 [256, 1024, 1024], P(('group', 'member')), may hold values from -1 to 4, as said below
- targets: bfloat16 [256, 1024], P(('group', 'member')), may hold values from -6 to 6
- queries: float32 [8, 4096], P(None, ('group', 'member')), may hold values from -4 to 4
- prior_precision: float32 [4096], P(('group', 'member')), may hold values from 0.05 to 0.2
- batch_order: int32 [4096], replicated, may hold values from 0 to 4095, each once
- noise: float32 [4096, 4096], P('group', 'member'), may hold values from -6 to 6
Outputs:
- samples: float32 [4096, 4096], P('group', 'member')
Inputs may be any that keep to these rules, and one draw needn't show every extreme that they name: `batch_order`: each query number appears exactly once. `inverse_cov`: each expert's matrix is symmetric positive definite.
All inputs are finite; a program needn't handle non-finite values.
Results may differ from a plain program's by a relative error of at most 0.0025.
Values sent between devices are 32-bit elements; how exact they have to be, the bound alone decides.
No kernel may reach another device: no remote copies, remote signals or barrier semaphores. Data moves between devices by JAX's collectives and lax.ppermute only.
A program may use at most 128 MiB of HBM per device.

v0:
```python
import jax
import jax.numpy as jnp
from jax import lax
from jax.sharding import Mesh
from jax.sharding import PartitionSpec as P

GROUP = ("group_0", "group_1")
GROUP_MEMBER = ("group_0", "group_1", "member")


kernel_rate = 0.25


def laid_out(pieces, dim):
    dims = list(pieces.shape[1:])
    dims[dim] *= pieces.shape[0]
    return jnp.moveaxis(pieces, 0, dim).reshape(dims)


def gather_packed(arrays, axis, dims):
    ravelled = jnp.concatenate([a.reshape(-1) for a in arrays])
    lines, at, finished = (lax.all_gather(ravelled, axis), 0, [])
    for a, dim in zip(arrays, dims):
        pieces = lines[:, at : at + a.size].reshape(-1, *a.shape)
        finished.append(laid_out(pieces, dim))
        at += a.size
    return tuple(finished)


def own_block(pieces, axes, sequence):
    inside = pieces.shape[1:]
    pieces = pieces.reshape(*(lax.axis_size(a) for a in axes), *inside)
    pieces = jnp.moveaxis(pieces, sequence, range(len(axes))).reshape(-1, *inside)
    for k in sequence:
        pieces = lax.psum_scatter(pieces, axes[k], scatter_dimension=0, tiled=True)
    return pieces[0]


def in_blocks(shard, dim, devices):
    dims = shard.shape
    pieces = shard.reshape(*dims[:dim], devices, dims[dim] // devices, *dims[dim + 1 :])
    return jnp.moveaxis(pieces, dim, 0)


def sum_by_axis(shard, axes, sequence, dim):
    devices = lax.axis_size(axes)
    return own_block(in_blocks(shard, dim, devices), axes, sequence)


def from_everyone(shard, axis):
    devices = lax.axis_size(axis)
    return lax.all_to_all(
        jnp.broadcast_to(shard[None], (devices, *shard.shape)), axis, 0, 0, tiled=True
    )


def of_everyone(shard, axis):
    return from_everyone(shard, axis).sum(axis=0)


def together(arrays, axis):
    ravelled, at, finished = (jnp.concatenate([a.reshape(-1) for a in arrays]), 0, [])
    subtotal = of_everyone(ravelled, axis)
    for a in arrays:
        finished.append(subtotal[at : at + a.size].reshape(a.shape))
        at += a.size
    return tuple(finished)


def kernel_rows(ordered, coords):
    inner = jnp.dot(
        ordered.T, coords, precision=lax.Precision.HIGHEST, preferred_element_type=jnp.float32
    )
    dist = (
        jnp.sum(ordered * ordered, axis=0)[:, None]
        + jnp.sum(coords * coords, axis=0)[None, :]
        - 2.0 * inner
    )
    return jnp.exp(-kernel_rate * dist).astype(jnp.bfloat16)


def per_device(points, inverse_cov, targets, queries, prior_precision, batch_order, noise):
    batch_size = noise.shape[0]
    groups = lax.axis_size(GROUP)
    members = lax.axis_size("member")
    all_queries, all_prior = gather_packed((queries, prior_precision), GROUP_MEMBER, (1, 0))
    ordered = jnp.take(all_queries, batch_order, axis=1)
    prior_sorted = jnp.take(all_prior, batch_order)
    count = points.shape[2]
    cross = kernel_rows(ordered, points[0])
    proj = jnp.dot(cross, inverse_cov[0], preferred_element_type=jnp.float32).astype(jnp.bfloat16)
    info_terms = jnp.dot(proj, targets[0], preferred_element_type=jnp.float32)
    terms = jnp.einsum(
        "bqm,bpm->bqp",
        proj.reshape(groups, batch_size, count),
        cross.reshape(groups, batch_size, count),
        preferred_element_type=jnp.float32,
    )
    main = terms.reshape(groups, batch_size * batch_size)
    info_rows = info_terms.reshape(groups, batch_size)
    group_index = lax.axis_index(GROUP)
    partial_rows, partial_info = (
        sum_by_axis(main, GROUP, (1, 0), 0),
        sum_by_axis(info_rows, GROUP, (1, 0), 0),
    )
    main_vec, info = together((partial_rows[0], partial_info[0]), "member")
    precision = main_vec.reshape(batch_size, batch_size)
    experts = points.shape[0] * groups * members
    prior_batch = lax.dynamic_slice_in_dim(prior_sorted, group_index * batch_size, batch_size)
    precision = precision / experts + prior_batch[:, None] * jnp.eye(batch_size, dtype=jnp.float32)
    info = (info / experts)[:, None]
    factor = jnp.linalg.cholesky(precision)
    forward = lax.linalg.triangular_solve(factor, info, left_side=True, lower=True)
    right_side = forward + noise
    return lax.linalg.triangular_solve(
        factor, right_side, left_side=True, lower=True, transpose_a=True
    )


def solution(mesh):
    finer = Mesh(mesh.devices.reshape(2, 8, mesh.shape["member"]), ("group_0", "group_1", "member"))
    in_specs = (
        P(GROUP_MEMBER, None, None),
        P(GROUP_MEMBER, None, None),
        P(GROUP_MEMBER, None),
        P(None, GROUP_MEMBER),
        P(GROUP_MEMBER),
        P(),
        P(GROUP, "member"),
    )
    out_specs = P(GROUP, "member")
    return jax.shard_map(
        per_device, mesh=finer, in_specs=in_specs, out_specs=out_specs, check_vma=False
    )
```

profile of v0, /device:TPU:1, one launch (start us, length us, event | category | flops | bytes accessed | tf_op | source)
XLA Modules:
  0.0 629.5 jit_solution(1989426724511906720)
XLA Ops:
  6.5 0.9 reshape.88
  7.5 0.8 maximum_dynamic-update-slice_fusion
  10.4 0.8 fusion.16
  11.2 251.8 %all-reduce.10.cloned.1.call-done = f32[36864]{0:T(1024)} async-done(((f32[36864]{0:T(1024)}), f32[36864]{0:T(1024)}) %all-reduce.10.cloned.1.call-update) | async-done | bytes 147472
  263.0 1.1 reshape.132
  264.2 2.5 copy.41
  266.7 15.7 %gather_fusion = f32[4096,8]{1,0:T(8,128)} fusion(f32[8,4096]{0,1:T(8,128)} %bitcast.96, s32[4096]{0:T(1024)S(1)} %fusion.17), kind=kCustom, calls=%fused_computation | custom fusion | bytes 278528 | tf_op jit(solution)/shard_map/jit(_take)/gather | solution.py:87
  282.3 2.5 multiply_reduce_fusion
  284.8 19.1 %exponential_convert_fusion = bf16[4096,1024]{1,0:T(8,128)(2,1)S(1)} fusion(f32[1024]{0:T(1024)S(1)} %fusion.16, f32[4096]{0:T(1024)S(1)} %multiply_reduce_fusion, f32[4096,8]{1,0:T(8,128)} %gather_fusion, pred[4096]{0:T(1024)(128)(4,1)S(1)} %compare_and_fusion, f32[1,8,1024]{2,1,0:T(8,128)} %param.7), kind=kOutput, calls=%fused_computation.4 | convolution fusion | flops 423657472 | bytes 8577024 | tf_op jit(solution)/shard_map/dot_general | solution.py:71
  303.9 10.8 %convolution_convert_fusion = bf16[4096,1024]{1,0:T(8,128)(2,1)} fusion(bf16[4096,1024]{1,0:T(8,128)(2,1)S(1)} %exponential_convert_fusion, bf16[1,1024,1024]{2,1,0:T(8,128)(2,1)S(1)} %copy-done), kind=kOutput, calls=%fused_computation.5 | convolution fusion | flops 8594128896 | bytes 18874368 | tf_op jit(solution)/shard_map/dot_general | solution.py:91
  314.8 10.1 %fusion.24 = f32[16,256,256]{2,1,0:T(8,128)} fusion(bf16[16,256,1024]{2,1,0:T(8,128)(2,1)} %bitcast.92, bf16[16,256,1024]{2,1,0:T(8,128)(2,1)} %bitcast.95), kind=kOutput, calls=%fused_computation.69 | convolution fusion | flops 2147483648 | bytes 20971520 | tf_op jit(solution)/shard_map/bqm,bpm->bqp/dot_general | solution.py:93
  324.8 4.4 reshape_reshape_reshape.4
  329.3 8.5 %copy.42 = f32[2,8,1,65536]{3,2,0,1:T(1,128)} copy(f32[2,8,1,65536]{3,1,0,2:T(8,128)} %reshape_reshape_reshape.4) | data formatting | bytes 8388608 | tf_op jit(solution)/shard_map/reshape;reshape;reshape | solution.py:32
  339.7 104.6 %all-reduce.12.cloned.1.call-done = f32[16,1,65536]{2,1,0:T(1,128)} async-done(((f32[16,1,65536]{2,1,0:T(1,128)}), f32[16,1,65536]{2,1,0:T(1,128)}) %all-reduce.12.cloned.1.call-update) | async-done | bytes 4194320
  444.2 1.9 constant_dynamic-slice_fusion.4
  446.2 5.6 fusion.18
  451.8 22.3 %all-reduce.4 = f32[16,1,256]{2,1,0:T(1,128)S(1)} all-reduce(f32[16,1,256]{2,1,0:T(1,128)S(1)} %bitcast.100), channel_id=5, replica_groups=mesh['group_0'=2,'group_1'=8,'member'=16] {'group_1'}, use_global_device_ids=true, to_apply=%region_4.5.clone | all-reduce | flops 4096 | bytes 32768
  474.2 5.3 all-reduce.5
  480.0 7.5 %all-reduce.14.cloned.1.call-done = f32[2,1,65536]{2,1,0:T(1,128)} async-done(((f32[2,1,65536]{2,1,0:T(1,128)}), f32[2,1,65536]{2,1,0:T(1,128)}) %all-reduce.14.cloned.1.call-update) | async-done | bytes 524304
  487.5 1.5 constant_dynamic-slice_fusion.3
  489.0 4.1 broadcast_in_dim.33
  493.2 5.7 all-to-all-start
  499.0 23.2 %gather_fusion.1 = f32[4096]{0:T(1024)S(1)} fusion(f32[4096]{0:T(1024)S(1)} %reshape.96, s32[4096]{0:T(1024)S(1)} %fusion.17), kind=kCustom, calls=%fused_computation.1 | custom fusion | bytes 49152 | tf_op jit(solution)/shard_map/jit(_take)/gather | solution.py:88
  522.3 32.6 %all-to-all-done = f32[16,1,65792]{2,1,0:T(1,128)} async-done(((f32[16,1,65792]{2,1,0:T(1,128)}), f32[16,1,65792]{2,1,0:T(1,128)}, u32[]{:S(2)}, u32[]{:S(2)}) %all-to-all-start) | async-done | bytes 4210720 | tf_op jit(solution)/shard_map/all_to_all | solution.py:52
  554.9 4.8 reduce_sum.29
  560.2 11.7 %cholesky.49 = f32[128,128]{1,0:T(8,128)S(1)} custom-call(f32[128,128]{1,0:T(8,128)S(1)} %cholesky.115), custom_call_target="Cholesky" | custom-call | tf_op jit(solution)/shard_map/jit(cholesky)/cholesky | solution.py:112
  572.0 9.8 %custom-call.16 = f32[1,128,128]{1,2,0:T(8,128)S(1)} custom-call(f32[1,128,128]{2,1,0:T(8,128)S(1)} %get-tuple-element.44), custom_call_target="InvertDiagBlocksLowerTriangular" | custom-call | tf_op jit(solution)/shard_map/jit(cholesky)/cholesky | solution.py:112
  582.4 11.9 %cholesky.103 = f32[128,128]{1,0:T(8,128)S(1)} custom-call(f32[128,128]{1,0:T(8,128)S(1)} %convolution_subtract_fusion.1), custom_call_target="Cholesky" | custom-call | tf_op jit(solution)/shard_map/jit(cholesky)/cholesky | solution.py:112
  596.6 4.3 while.1
  597.3 1.3 dynamic-slice.19
  599.4 1.3 dynamic-slice.19
  600.9 19.7 %custom-call.17 = f32[2,128,128]{1,2,0:T(8,128)S(1)} custom-call(f32[2,128,128]{2,1,0:T(8,128)S(1)} %get-tuple-element.12), custom_call_target="InvertDiagBlocksLowerTriangular" | custom-call | tf_op jit(solution)/shard_map/triangular_solve | solution.py:115
  (75 shorter events, 10.1 us)
Async XLA Ops:
  6.5 297.4 %copy-start = (bf16[1,1024,1024]{2,1,0:T(8,128)(2,1)S(1)}, bf16[1,1024,1024]{2,1,0:T(8,128)(2,1)}, u32[]{:S(2)}) copy-start(bf16[1,1024,1024]{2,1,0:T(8,128)(2,1)} %param.8) | copy-start | bytes 6291460
  6.5 256.4 %all-reduce.10.cloned.1.call-start = ((), (), s32[]{:S(2)}) async-start(), calls=%async_computation.1 | async-start | bytes 294912
  8.3 0.7 copy-start.2
  8.9 435.3 %all-reduce.12.cloned.1.call-start = ((), (), s32[]{:S(2)}) async-start(), calls=%async_computation.2 | async-start | bytes 8388608
  303.9 10.9 %copy-start.1 = (bf16[4096,1024]{1,0:T(8,128)(2,1)}, bf16[4096,1024]{1,0:T(8,128)(2,1)S(1)}, u32[]{:S(2)}) copy-start(bf16[4096,1024]{1,0:T(8,128)(2,1)S(1)} %exponential_convert_fusion) | copy-start | bytes 25165828
  329.2 8.6 %copy-start.6 = (u32[256]{0:T(256)S(1)}, u32[256]{0:T(256)}, u32[]{:S(2)}) copy-start(u32[256]{0:T(256)} %constant.168) | copy-start | bytes 3076
  329.3 9.2 %copy-start.5 = (u32[256]{0:T(256)S(1)}, u32[256]{0:T(256)}, u32[]{:S(2)}) copy-start(u32[256]{0:T(256)} %constant.164) | copy-start | bytes 3076
  329.3 116.9 %copy-start.4 = (bf16[1,1024]{1,0:T(2,128)(2,1)S(1)}, bf16[1,1024]{1,0:T(2,128)(2,1)}, u32[]{:S(2)}) copy-start(bf16[1,1024]{1,0:T(2,128)(2,1)} %param.9) | copy-start | bytes 6148
  337.8 149.7 %all-reduce.14.cloned.1.call-start = ((), (), s32[]{:S(2)}) async-start(), calls=%async_computation.3 | async-start | bytes 1048576
  493.2 61.7 %all-to-all-start = ((f32[16,1,65792]{2,1,0:T(1,128)}), f32[16,1,65792]{2,1,0:T(1,128)}, u32[]{:S(2)}, u32[]{:S(2)}) async-start(f32[16,1,65792]{2,1,0:T(1,128)} %broadcast_in_dim.33), calls=%async_computation | async-start | bytes 8421376 | tf_op jit(solution)/shard_map/all_to_all | solution.py:52
  522.2 98.9 %copy-start.3 = (f32[256,256]{1,0:T(8,128)S(1)}, f32[256,256]{1,0:T(8,128)}, u32[]{:S(2)}) copy-start(f32[256,256]{1,0:T(8,128)} %param.13) | copy-start | bytes 786436
Sparse Core Ops, SparseCore 0:
  12.8 250.1 all-reduce.9
  337.9 106.2 all-reduce.11
  446.8 40.6 all-reduce.13
where the time goes:
time: 640 us; the launch traced here: 629 us
  waiting for transfers between devices  396 us (62%)
  local copies, waits for them, and re-layouts  71.4 us (11%)
  other arithmetic  65.2 us (10%)
  matrix products  47.4 us (7%)
  blocking collectives  27.6 us (4%)
  between operations  15.6 us (2%)
    unnamed x6, waiting for transfers between devices  364 us
    another operation x6, other arithmetic, per_device(): factor = jnp.linalg.cholesky(precision)  34.2 us
    all_to_all x1, waiting for transfers between devices, from_everyone(): lax.all_to_all(jnp.broadcast_to(shard[None], (devices, *shard.shape)), ax...  32.6 us
    unnamed x2, blocking collectives  27.6 us
    gather x1, local copies, waits for them, and re-layouts, per_device(): prior_sorted = jnp.take(all_prior, batch_order)  23.2 us
    another operation x4, other arithmetic, per_device(): lax.linalg.triangular_solve(factor, right_side, left_side=True, lower=Tru...  20.4 us
    dot_general x1, matrix products, kernel_rows(): jnp.dot(ordered.T, coords, precision=lax.Precision.HIGHEST, preferred_ele...  19.1 us
    gather x1, local copies, waits for them, and re-layouts, per_device(): ordered = jnp.take(all_queries, batch_order, axis=1)  15.7 us
  transfers between devices with their start and end apart: 4, of which 4 were waited for; matrix products, arithmetic and copies ran while one was open for 5% of the time, Pallas kernels for 0%

commit v1 on v0

v1 whole, which is shorter than its diff:
```python
import jax
import jax.numpy as jnp
from jax import lax
from jax.experimental import pallas as pl
from jax.experimental.pallas import tpu as pltpu
from jax.sharding import Mesh
from jax.sharding import PartitionSpec as P

AXES = ("yh", "z", "yl", "x", "c")
GROUP = ("yh", "z")
MEMBER = ("yl", "x", "c")
RATE = 0.25
F32, BF16 = jnp.float32, jnp.bfloat16


def iota(shape, dim):
    return lax.broadcasted_iota(jnp.int32, shape, dim)


def dot(a, b, dims):
    return lax.dot_general(a, b, (dims, ((), ())), preferred_element_type=F32)


def three_parts(v):
    a = v.astype(BF16).astype(F32)
    b = (v - a).astype(BF16).astype(F32)
    return a, b, (v - a - b)


def expert_kernel(me_ref, order_ref, table_ref, points_ref, inv_ref, targets_ref,
                  own_ref, other_ref, parts_s, fold_s, points_s, cross_s):
    b = pl.program_id(0)

    @pl.when(b == 0)
    def _():
        table = table_ref[:, 0:128].T
        parts_s[...] = jnp.concatenate(three_parts(table), axis=0).astype(BF16)
        fold_s[...] = (iota((32, 384), 1) // 16 == iota((32, 384), 0)).astype(F32).astype(BF16)
        p = points_ref[0]
        norm = -RATE * jnp.sum(p * p, axis=0, keepdims=True)
        h, m, l = three_parts(2.0 * RATE * p)
        one = jnp.ones((3, p.shape[1]), F32)
        tail = jnp.concatenate([one, *three_parts(norm), jnp.zeros((2, p.shape[1]), F32)], axis=0)
        points_s[...] = jnp.concatenate([h, m, l, h, m, l, h, m, l, tail], axis=0).astype(BF16)
        cross_s[256:272, :] = jnp.where(
            iota((16, 1024), 0) == 0, jnp.broadcast_to(targets_ref[...].astype(F32), (16, 1024)), 0.0
        ).astype(BF16)

    o = order_ref[pl.ds(b, 1), :]
    hi = lax.shift_right_logical(o, 4)
    row = (hi & 128) | ((hi & 7) << 4) | (lax.shift_right_logical(hi, 3) & 15)
    hot = jnp.where(iota((256, 256), 0) == row, 1.0, 0.0).astype(BF16)
    picked = dot(parts_s[...], hot, ((1,), (0,)))
    picked = jnp.where((iota((384, 256), 0) & 15) == (o & 15), picked, 0.0).astype(BF16)
    q = dot(fold_s[...], picked, ((1,), (0,)))
    h, m, l = q[0:8], q[8:16], q[16:24]
    full = (h + m) + l
    norm = -RATE * jnp.sum(full * full, axis=0, keepdims=True)
    tail = jnp.concatenate([*three_parts(norm), jnp.ones((3, 256), F32), jnp.zeros((2, 256), F32)], axis=0)
    left = jnp.concatenate([h, h, h, m, m, m, l, l, l, tail], axis=0).T.astype(BF16)
    power = dot(left, points_s[...], ((1,), (0,)))
    cross_s[0:256, :] = jnp.exp(power).astype(BF16)
    proj = dot(cross_s[0:256, :], inv_ref[0], ((1,), (0,))).astype(BF16)
    terms = dot(cross_s[...], proj, ((1,), (1,)))
    low = iota((128, 128), 0) - iota((128, 128), 1)
    first = terms[0:128, 0:128]
    mixed = jnp.where(low > 0, first, terms[128:256, 128:256])
    diag = jnp.sum(jnp.where(low == 0, first, 0.0), axis=0, keepdims=True)
    info = terms[256:257, :]
    extra = jnp.concatenate([diag, info[:, 0:128], info[:, 128:256], jnp.zeros((13, 128), F32)], axis=0)
    core = me_ref[0]
    start = (b // 8) * 1088 + (b % 8) * 17
    for r in range(17):
        if r < 8:
            rows = terms[128 + 16 * r : 144 + 16 * r, 0:128]
        elif r < 16:
            rows = mixed[16 * (r - 8) : 16 * (r - 7), :]
        else:
            rows = extra
        a, c = rows[0:8], rows[8:16]
        own_ref[pl.ds(start + r, 8, stride=136), :] = jnp.where(core == 0, a, c)
        other_ref[pl.ds(start + r, 8, stride=136), :] = jnp.where(core == 0, c, a)


def expert_terms(core, order, table, points, inverse_cov, targets):
    whole = lambda *shape: pl.BlockSpec(shape, lambda b, me: (0,) * len(shape))
    return pl.pallas_call(
        expert_kernel,
        out_shape=(jax.ShapeDtypeStruct((2176, 128), F32),) * 2,
        grid_spec=pltpu.PrefetchScalarGridSpec(
            num_scalar_prefetch=1,
            grid=(16,),
            in_specs=[whole(16, 256), whole(256, 144), whole(1, 8, 1024), whole(1, 1024, 1024), whole(1, 1024)],
            out_specs=(whole(2176, 128),) * 2,
            scratch_shapes=[
                pltpu.VMEM((384, 256), BF16),
                pltpu.VMEM((32, 384), BF16),
                pltpu.VMEM((80, 1024), BF16),
                pltpu.VMEM((272, 1024), BF16),
            ],
        ),
        compiler_params=pltpu.CompilerParams(
            dimension_semantics=("arbitrary",), vmem_limit_bytes=40 << 20
        ),
        name="expert",
    )(core, order, table, points, inverse_cov, targets)


def from_everyone(v, axes, n):
    return lax.all_to_all(jnp.broadcast_to(v[None], (n, *v.shape)), axes, 0, 0, tiled=True)


def per_device(points, inverse_cov, targets, queries, prior_precision, batch_order, noise):
    mine = jnp.concatenate([queries.reshape(-1), prior_precision])
    table = from_everyone(mine, ("z", "yl"), 16)
    table = from_everyone(table, ("yh", "x", "c"), 16).reshape(256, 144)
    order = batch_order.reshape(16, 256)
    core = lax.axis_index("c")
    own, other = expert_terms(core[None], order, table, points, inverse_cov, targets)
    own = own + lax.ppermute(other, "c", [(0, 1), (1, 0)])
    part = lax.all_to_all(own.reshape(16, 136, 128), ("yh", "x", "yl"), 0, 0, tiled=True).sum(0)
    part = part.reshape(8, 1, 17 * 128)
    part = jnp.broadcast_to(part, (8, 2, 17 * 128)).reshape(16, 17 * 128)
    part = lax.all_to_all(part, ("z", "yl"), 0, 0, tiled=True).reshape(8, 2 * 17 * 128).sum(0)
    pieces = from_everyone(part, ("c", "x"), 8).reshape(16, 17, 128)

    packed = jnp.moveaxis(pieces, 0, 1).reshape(272, 128) / 256.0
    mixed = packed[128:256]
    first = jnp.tril(mixed, -1) + jnp.diag(packed[256]) + jnp.tril(mixed, -1).T
    second = jnp.triu(mixed) + jnp.triu(mixed, 1).T
    corner = packed[0:128]
    precision = jnp.block([[first, corner.T], [corner, second]])
    info = packed[257:259].reshape(256, 1)
    group = lax.axis_index(GROUP)
    o = lax.dynamic_index_in_dim(order, group, 0, keepdims=False)
    hi = o >> 4
    row = (hi & 128) | ((hi & 7) << 4) | ((hi >> 3) & 15)
    prior = table[:, 128:][row, o & 15]
    precision = precision + jnp.diag(prior)
    factor = jnp.linalg.cholesky(precision)
    forward = lax.linalg.triangular_solve(factor, info, left_side=True, lower=True)
    return lax.linalg.triangular_solve(
        factor, forward + noise, left_side=True, lower=True, transpose_a=True
    )


def solution(mesh):
    finer = Mesh(mesh.devices.reshape(2, 8, 2, 4, 2), AXES)
    in_specs = (
        P(AXES, None, None),
        P(AXES, None, None),
        P(AXES, None),
        P(None, AXES),
        P(AXES),
        P(),
        P(GROUP, MEMBER),
    )
    return jax.shard_map(
        per_device, mesh=finer, in_specs=in_specs, out_specs=P(GROUP, MEMBER), check_vma=False
    )
```

time: 640 us -> 178 us (0.28); the launches traced: 629 us -> 177 us
  waiting for transfers between devices: 396 us -> 22.1 us
  local copies, waits for them, and re-layouts: 71.4 us -> 14.1 us
  matrix products: 47.4 us -> 1.75 us
  Pallas kernels: 0 us -> 25 us
  between operations: 15.6 us -> 1.61 us
  starting transfers between devices: 5.77 us -> 19 us
  blocking collectives: 27.6 us -> 37.2 us
  other arithmetic: 65.2 us -> 56.5 us
    unnamed x6 -> x0, waiting for transfers between devices: 364 us -> none
    dot_general x4 -> x0, matrix products: 45.6 us -> none  [the longest x1 19.1 us: kernel_rows(): jnp.dot(ordered.T, coords, precision=lax.Precision.HIGHEST, preferred_ele...]
    all_to_all x0 -> x2, blocking collectives: none -> 37.2 us  [the longest x1 19.9 us: per_device(): lax.all_to_all(own.reshape(16, 136, 128), ('yh', 'x', 'yl'), 0, 0, tiled=...]
    gather x2 -> x1, local copies, waits for them, and re-layouts: 38.9 us -> 1.95 us  [per_device(): prior = table[:, 128:][row, o & 15]]
    unnamed x2 -> x0, blocking collectives: 27.6 us -> none
    pallas_call x0 -> x1, Pallas kernels: none -> 25 us  [expert_terms(): pl.pallas_call(expert_kernel, out_shape=(jax.ShapeDtypeStruct((2176, 128)...]
    another operation x13 -> x11, local copies, waits for them, and re-layouts: 17.1 us -> 4.05 us  [the longest x2 12.9 us: own_block(): pieces = pieces.reshape(*(lax.axis_size(a) for a in axes), *inside)]
    all_to_all x1 -> x3, waiting for transfers between devices: 32.6 us -> 19.7 us  [the longest x2 11.1 us: from_everyone(): lax.all_to_all(jnp.broadcast_to(v[None], (n, *v.shape)), axes, 0, 0, tile...]
  transfers between devices with their start and end apart: 4 -> 4, of which waited for: 4 -> 4; matrix products, arithmetic and copies ran while one was open for 5% -> 2% of each run, Pallas kernels for 0% -> 0%
where the time goes in v1:
time: 178 us; the launch traced here: 177 us
  other arithmetic  56.5 us (32%)
  blocking collectives  37.2 us (21%)
  Pallas kernels  25 us (14%)
  waiting for transfers between devices  22.1 us (12%)
  starting transfers between devices  19 us (11%)
  local copies, waits for them, and re-layouts  14.1 us (8%)
    another operation x6, other arithmetic, per_device(): factor = jnp.linalg.cholesky(precision)  33.9 us
    pallas_call x1, Pallas kernels, expert_terms(): pl.pallas_call(expert_kernel, out_shape=(jax.ShapeDtypeStruct((2176, 128)...  25 us
    another operation x4, other arithmetic, per_device(): lax.linalg.triangular_solve(factor, forward + noise, left_side=True, lowe...  20.7 us
    all_to_all x1, blocking collectives, per_device(): lax.all_to_all(own.reshape(16, 136, 128), ('yh', 'x', 'yl'), 0, 0, tiled=...  19.9 us
    all_to_all x1, blocking collectives, from_everyone(): lax.all_to_all(jnp.broadcast_to(v[None], (n, *v.shape)), axes, 0, 0, tile...  17.3 us
    all_to_all x2, starting transfers between devices, from_everyone(): lax.all_to_all(jnp.broadcast_to(v[None], (n, *v.shape)), axes, 0, 0, tile...  14.7 us
    all_to_all x2, waiting for transfers between devices, from_everyone(): lax.all_to_all(jnp.broadcast_to(v[None], (n, *v.shape)), axes, 0, 0, tile...  11.1 us
    all_to_all x1, waiting for transfers between devices, per_device(): lax.all_to_all(part, ('z', 'yl'), 0, 0, tiled=True).reshape(8, 2 * 17 * 128)  8.63 us
  transfers between devices with their start and end apart: 4, of which 4 were waited for; matrix products, arithmetic and copies ran while one was open for 2% of the time, Pallas kernels for 0%

profile of v1, /device:TPU:1, one launch (start us, length us, event | category | flops | bytes accessed | tf_op | source)
XLA Modules:
  0.0 177.4 jit_solution(7024141445532126246)
XLA Ops:
  0.0 0.8 reshape.160
  0.8 0.7 pad_maximum_fusion.2
  1.4 17.3 %all_to_all.31 = f32[16,1,144]{2,1,0:T(1,128)S(1)} all-to-all(f32[16,1,144]{2,1,0:T(1,128)S(1)} %broadcast_in_dim.80), channel_id=1, replica_groups=mesh['yh'=2,'z'=8,'yl'=2,'x'=4,'c'=2] {'z','yl'}, dimensions={0} | all-to-all | bytes 18432 | tf_op jit(solution)/shard_map/all_to_all | solution.py:110
  18.8 0.7 broadcast_in_dim.82
  19.5 8.8 %all-to-all-start.1 = ((f32[16,16,144]{2,1,0:T(8,128)}), f32[16,16,144]{2,1,0:T(8,128)S(1)}, u32[]{:S(2)}, u32[]{:S(2)}) async-start(f32[16,16,144]{2,1,0:T(8,128)} %broadcast_in_dim.82), calls=%async_computation.1 | async-start | bytes 524288 | tf_op jit(solution)/shard_map/all_to_all | solution.py:110
  28.3 0.7 reshape.159.order_ref
  29.0 8.0 %all-to-all-done.1 = f32[16,16,144]{2,1,0:T(8,128)S(1)} async-done(((f32[16,16,144]{2,1,0:T(8,128)}), f32[16,16,144]{2,1,0:T(8,128)S(1)}, u32[]{:S(2)}, u32[]{:S(2)}) %all-to-all-start.1) | async-done | bytes 147488 | tf_op jit(solution)/shard_map/all_to_all | solution.py:110
  37.0 1.6 copy-done
  38.6 0.8 copy-done.1
  39.3 0.7 copy-done.2
  40.0 25.0 %expert.1 = (f32[2176,128]{1,0:T(8,128)S(1)}, f32[2176,128]{1,0:T(8,128)S(1)}) custom-call(s32[1]{0:T(128)} %bitcast.me_ref, s32[16,256]{1,0:T(8,128)S(1)} %reshape.159.order_ref, f32[256,144]{1,0:T(8,128)S(1)} %bitcast.81, f32[1,8,1024]{2,1,0:T(8,128)S(1)} %copy-done.1, bf16[1,1024,1024]{2,1,0:T(8,128)(2,1)S(1)} %copy-done, bf16[1,1024]{1,0:T(2,128)(2,1)S(1)} %copy-done.2), custom_call_target="tpu_custom_call" | custom-call | tf_op jit(solution)/shard_map/expert/pallas_call | solution.py:87
  65.1 0.8 collective-permute-start
  65.9 2.4 %collective-permute-done = f32[2176,128]{1,0:T(8,128)S(1)} collective-permute-done((f32[2176,128]{1,0:T(8,128)S(1)}, f32[2176,128]{1,0:T(8,128)S(1)}, u32[]{:S(2)}, u32[]{:S(2)}) %collective-permute-start) | collective-permute-done | bytes 1114144 | tf_op jit(solution)/shard_map/ppermute | solution.py:120
  68.4 19.9 %all_to_all.32 = f32[16,136,128]{2,1,0:T(8,128)S(1)} all-to-all(f32[16,136,128]{2,1,0:T(8,128)S(1)} %bitcast.84), channel_id=1, replica_groups=mesh['yh'=2,'z'=8,'yl'=2,'x'=4,'c'=2] {'yh','x','yl'}, dimensions={0} | all-to-all | bytes 2228224 | tf_op jit(solution)/shard_map/all_to_all | solution.py:121
  88.4 0.9 all_to_all.23
  89.3 3.5 %all-to-all-start.3 = ((f32[16,1,2176]{2,1,0:T(1,128)}), f32[16,1,2176]{2,1,0:T(1,128)S(1)}, u32[]{:S(2)}, u32[]{:S(2)}) async-start(f32[16,1,2176]{2,1,0:T(1,128)} %all_to_all.23), calls=%async_computation.3 | async-start | bytes 278528 | tf_op jit(solution)/shard_map/all_to_all | solution.py:124
  92.8 8.6 %all-to-all-done.3 = f32[16,1,2176]{2,1,0:T(1,128)S(1)} async-done(((f32[16,1,2176]{2,1,0:T(1,128)}), f32[16,1,2176]{2,1,0:T(1,128)S(1)}, u32[]{:S(2)}, u32[]{:S(2)}) %all-to-all-start.3) | async-done | bytes 139296 | tf_op jit(solution)/shard_map/all_to_all | solution.py:124
  101.9 0.7 broadcast_in_dim.85
  102.6 5.9 %all-to-all-start.4 = ((f32[8,1,4352]{2,1,0:T(1,128)}), f32[8,1,4352]{2,1,0:T(1,128)S(1)}, u32[]{:S(2)}, u32[]{:S(2)}) async-start(f32[8,1,4352]{2,1,0:T(1,128)} %broadcast_in_dim.85), calls=%async_computation.4 | async-start | bytes 278528 | tf_op jit(solution)/shard_map/all_to_all | solution.py:110
  108.7 1.9 %gather_fusion = f32[256]{0:T(256)S(1)} fusion(f32[256,16]{1,0:T(8,128)S(1)} %slice.97, s32[256]{0:T(256)S(1)} %bitcast.83), kind=kCustom, calls=%fused_computation | custom fusion | bytes 4096 | tf_op jit(solution)/shard_map/gather | solution.py:138
  110.6 3.1 %all-to-all-done.4 = f32[8,1,4352]{2,1,0:T(1,128)S(1)} async-done(((f32[8,1,4352]{2,1,0:T(1,128)}), f32[8,1,4352]{2,1,0:T(1,128)S(1)}, u32[]{:S(2)}, u32[]{:S(2)}) %all-to-all-start.4) | async-done | bytes 139296 | tf_op jit(solution)/shard_map/all_to_all | solution.py:110
  115.2 11.7 %cholesky.54 = f32[128,128]{1,0:T(8,128)S(1)} custom-call(f32[128,128]{1,0:T(8,128)S(1)} %cholesky.119), custom_call_target="Cholesky" | custom-call | tf_op jit(solution)/shard_map/jit(cholesky)/cholesky | solution.py:140
  127.0 9.8 %custom-call.16 = f32[1,128,128]{1,2,0:T(8,128)S(1)} custom-call(f32[1,128,128]{2,1,0:T(8,128)S(1)} %get-tuple-element.46), custom_call_target="InvertDiagBlocksLowerTriangular" | custom-call | tf_op jit(solution)/shard_map/jit(cholesky)/cholesky | solution.py:140
  137.4 11.7 %cholesky.107 = f32[128,128]{1,0:T(8,128)S(1)} custom-call(f32[128,128]{1,0:T(8,128)S(1)} %convolution_subtract_fusion.1), custom_call_target="Cholesky" | custom-call | tf_op jit(solution)/shard_map/jit(cholesky)/cholesky | solution.py:140
  149.3 0.6 compare_reduce_fusion
  151.3 4.0 %while.1 = (s32[]{:T(128)}, f32[256,256]{0,1:T(8,128)S(1)}, s32[2,2]{1,0:T(2,128)S(1)}, f32[2,128,128]{2,1,0:T(8,128)S(1)}, s32[]{:T(128)}) while((s32[]{:T(128)}, f32[256,256]{0,1:T(8,128)S(1)}, s32[2,2]{1,0:T(2,128)S(1)}, f32[2,128,128]{2,1,0:T(8,128)S(1)}, s32[]{:T(128)}) %tuple.26), condition=%wide.while_cond, body=%wide.while_body.sunk | while | flops 2 | bytes 393329 | solution.py:142
  151.3 0.6 fusion.25
  151.9 1.3 dynamic-slice.7
  153.3 0.6 fusion.25
  153.9 1.3 dynamic-slice.7
  155.3 19.9 %custom-call.17 = f32[2,128,128]{1,2,0:T(8,128)S(1)} custom-call(f32[2,128,128]{2,1,0:T(8,128)S(1)} %get-tuple-element.16), custom_call_target="InvertDiagBlocksLowerTriangular" | custom-call | tf_op jit(solution)/shard_map/triangular_solve | solution.py:142
  176.7 0.7 pad_maximum_fusion
  (68 shorter events, 4.7 us)
Async XLA Ops:
  19.5 17.5 %all-to-all-start.1 = ((f32[16,16,144]{2,1,0:T(8,128)}), f32[16,16,144]{2,1,0:T(8,128)S(1)}, u32[]{:S(2)}, u32[]{:S(2)}) async-start(f32[16,16,144]{2,1,0:T(8,128)} %broadcast_in_dim.82), calls=%async_computation.1 | async-start | bytes 524288 | tf_op jit(solution)/shard_map/all_to_all | solution.py:110
  37.0 1.6 copy-start
  38.6 0.8 copy-start.1
  39.3 0.7 copy-start.2
  65.1 3.2 %collective-permute-start = (f32[2176,128]{1,0:T(8,128)S(1)}, f32[2176,128]{1,0:T(8,128)S(1)}, u32[]{:S(2)}, u32[]{:S(2)}) collective-permute-start(f32[2176,128]{1,0:T(8,128)S(1)} %get-tuple-element.8), channel_id=1, source_target_pairs={{0,1},{1,0},{2,3},{3,2},{4,5},{5,4},{6,7},{7,6},{8,9},{9,8},{10,11... | collective-permute-start | bytes 3342344 | tf_op jit(solution)/shard_map/ppermute | solution.py:120
  89.3 12.2 %all-to-all-start.3 = ((f32[16,1,2176]{2,1,0:T(1,128)}), f32[16,1,2176]{2,1,0:T(1,128)S(1)}, u32[]{:S(2)}, u32[]{:S(2)}) async-start(f32[16,1,2176]{2,1,0:T(1,128)} %all_to_all.23), calls=%async_computation.3 | async-start | bytes 278528 | tf_op jit(solution)/shard_map/all_to_all | solution.py:124
  102.6 11.1 %all-to-all-start.4 = ((f32[8,1,4352]{2,1,0:T(1,128)}), f32[8,1,4352]{2,1,0:T(1,128)S(1)}, u32[]{:S(2)}, u32[]{:S(2)}) async-start(f32[8,1,4352]{2,1,0:T(1,128)} %broadcast_in_dim.85), calls=%async_computation.4 | async-start | bytes 278528 | tf_op jit(solution)/shard_map/all_to_all | solution.py:110
  151.3 24.5 %copy-start.3 = (f32[256,256]{1,0:T(8,128)S(1)}, f32[256,256]{1,0:T(8,128)}, u32[]{:S(2)}) copy-start(f32[256,256]{1,0:T(8,128)} %param.13) | copy-start | bytes 786436

commit v2 on v1

--- a/solution.py
+++ b/solution.py
@@ -33,9 +33,9 @@
 
     @pl.when(b == 0)
     def _():
-        table = table_ref[:, 0:128].T
-        parts_s[...] = jnp.concatenate(three_parts(table), axis=0).astype(BF16)
-        fold_s[...] = (iota((32, 384), 1) // 16 == iota((32, 384), 0)).astype(F32).astype(BF16)
+        parts_s[0:384, :] = jnp.concatenate(three_parts(table_ref[:, 0:128].T), axis=0).astype(BF16)
+        parts_s[384:432, :] = jnp.concatenate(three_parts(table_ref[:, 128:144].T), axis=0).astype(BF16)
+        fold_s[...] = (iota((32, 432), 1) // 16 == iota((32, 432), 0)).astype(F32).astype(BF16)
         p = points_ref[0]
         norm = -RATE * jnp.sum(p * p, axis=0, keepdims=True)
         h, m, l = three_parts(2.0 * RATE * p)
@@ -51,10 +51,11 @@
     row = (hi & 128) | ((hi & 7) << 4) | (lax.shift_right_logical(hi, 3) & 15)
     hot = jnp.where(iota((256, 256), 0) == row, 1.0, 0.0).astype(BF16)
     picked = dot(parts_s[...], hot, ((1,), (0,)))
-    picked = jnp.where((iota((384, 256), 0) & 15) == (o & 15), picked, 0.0).astype(BF16)
+    picked = jnp.where((iota((432, 256), 0) & 15) == (o & 15), picked, 0.0).astype(BF16)
     q = dot(fold_s[...], picked, ((1,), (0,)))
     h, m, l = q[0:8], q[8:16], q[16:24]
     full = (h + m) + l
+    prior = (q[24:25] + q[25:26]) + q[26:27]
     norm = -RATE * jnp.sum(full * full, axis=0, keepdims=True)
     tail = jnp.concatenate([*three_parts(norm), jnp.ones((3, 256), F32), jnp.zeros((2, 256), F32)], axis=0)
     left = jnp.concatenate([h, h, h, m, m, m, l, l, l, tail], axis=0).T.astype(BF16)
@@ -64,8 +65,9 @@
     terms = dot(cross_s[...], proj, ((1,), (1,)))
     low = iota((128, 128), 0) - iota((128, 128), 1)
     first = terms[0:128, 0:128]
-    mixed = jnp.where(low > 0, first, terms[128:256, 128:256])
-    diag = jnp.sum(jnp.where(low == 0, first, 0.0), axis=0, keepdims=True)
+    second = terms[128:256, 128:256] + jnp.where(low == 0, prior[:, 128:256], 0.0)
+    mixed = jnp.where(low > 0, first, second)
+    diag = jnp.sum(jnp.where(low == 0, first, 0.0), axis=0, keepdims=True) + prior[:, 0:128]
     info = terms[256:257, :]
     extra = jnp.concatenate([diag, info[:, 0:128], info[:, 128:256], jnp.zeros((13, 128), F32)], axis=0)
     core = me_ref[0]
@@ -93,8 +95,8 @@
             in_specs=[whole(16, 256), whole(256, 144), whole(1, 8, 1024), whole(1, 1024, 1024), whole(1, 1024)],
             out_specs=(whole(2176, 128),) * 2,
             scratch_shapes=[
-                pltpu.VMEM((384, 256), BF16),
-                pltpu.VMEM((32, 384), BF16),
+                pltpu.VMEM((432, 256), BF16),
+                pltpu.VMEM((32, 432), BF16),
                 pltpu.VMEM((80, 1024), BF16),
                 pltpu.VMEM((272, 1024), BF16),
             ],
@@ -104,6 +106,108 @@
         ),
         name="expert",
     )(core, order, table, points, inverse_cov, targets)
+
+
+def exact_dot(a, b, dims):
+    return lax.dot_general(
+        a, b, (dims, ((), ())), precision=lax.Precision.HIGHEST, preferred_element_type=F32
+    )
+
+
+def along_lanes(v, i):
+    return jnp.broadcast_to(v[:, i : i + 1], (8, 128))
+
+
+def along_rows(v, i):
+    return jnp.broadcast_to(v[i : i + 1, :], (8, 128))
+
+
+def factor_block(groups, done_ref):
+    for p in range(8):
+        g = groups[p]
+        cols = [along_lanes(g, 8 * p + j) for j in range(8)]
+        b = [[along_rows(cols[j], i) for j in range(i + 1)] for i in range(8)]
+        rows = [along_rows(g, i) for i in range(8)]
+        ahead = [[along_lanes(groups[t], 8 * p + j) for j in range(8)] for t in range(p + 1, 8)]
+        for k in range(8):
+            r = lax.rsqrt(b[k][k])
+            for i in range(k + 1, 8):
+                b[i][k] = b[i][k] * r
+            for i in range(k + 1, 8):
+                for j in range(k + 1, i + 1):
+                    b[i][j] = b[i][j] - b[i][k] * b[j][k]
+            rows[k] = rows[k] * r
+            for i in range(k + 1, 8):
+                rows[i] = rows[i] - b[i][k] * rows[k]
+            for t in range(p + 1, 8):
+                c = ahead[t - p - 1]
+                c[k] = c[k] * r
+                for j in range(k + 1, 8):
+                    c[j] = c[j] - c[k] * b[j][k]
+                groups[t] = groups[t] - c[k] * rows[k]
+            done_ref[8 * p + k : 8 * p + k + 1, :] = rows[k][0:1]
+
+
+def solve_kernel(pieces_ref, noise_ref, out_ref, aug_s, done_s, inverse_s):
+    scale = 1.0 / 256.0
+
+    def packed(r):
+        return jnp.concatenate(
+            [pieces_ref[pl.ds(r, 8, stride=17), :], pieces_ref[pl.ds(136 + r, 8, stride=17), :]], axis=0
+        ) * scale
+
+    corner = jnp.concatenate([packed(r) for r in range(8)], axis=0)
+    mixed = jnp.concatenate([packed(r) for r in range(8, 16)], axis=0)
+    extra = packed(16)
+    flipped = mixed.T
+    low = iota((128, 128), 0) - iota((128, 128), 1)
+    first = jnp.where(low > 0, mixed, jnp.where(low < 0, flipped, jnp.broadcast_to(extra[0:1], (128, 128))))
+    second = jnp.where(low > 0, flipped, mixed)
+    aug_s[0:128, 0:128] = first
+    aug_s[0:128, 128:256] = corner.T
+    aug_s[128:256, 0:128] = corner
+    aug_s[128:256, 128:256] = second
+    aug_s[:, 256:512] = jnp.where(iota((256, 256), 0) == iota((256, 256), 1), 1.0, 0.0)
+    inverse_s[...] = jnp.zeros((256, 256), F32)
+    lane = iota((64, 128), 1)
+    unit = jnp.where(iota((64, 128), 0) + 64 == lane, 1.0, 0.0)
+    for s in range(4):
+        top, tile = 64 * s, 128 * (s // 2)
+        block = aug_s[top : top + 64, tile : tile + 128]
+        if s % 2:
+            block = pltpu.roll(block, 64, 1)
+        block = jnp.where(lane < 64, block, unit)
+        factor_block([block[8 * t : 8 * t + 8] for t in range(8)], done_s)
+        inv = pltpu.roll(done_s[...], 64, 1)[:, 0:64]
+        wide = 128 * (s // 2 + 1)
+        inverse = exact_dot(inv, aug_s[top : top + 64, 256 : 256 + wide], ((1,), (0,)))
+        inverse_s[top : top + 64, 0:wide] = inverse
+        if s < 3:
+            begin = 128 * ((s + 1) // 2)
+            upper = exact_dot(inv, aug_s[top : top + 64, begin:256], ((1,), (0,)))
+            lower = upper.T[top + 64 - begin :]
+            rest = slice(top + 64, 256)
+            aug_s[rest, begin:256] = aug_s[rest, begin:256] - exact_dot(lower, upper, ((1,), (0,)))
+            aug_s[rest, 256 : 256 + wide] = aug_s[rest, 256 : 256 + wide] - exact_dot(
+                lower, inverse, ((1,), (0,))
+            )
+    info = jnp.concatenate([extra[1:2], extra[2:3]], axis=1)
+    inverse = inverse_s[...]
+    forward = jnp.sum(inverse * info, axis=1, keepdims=True)
+    out_ref[...] = exact_dot(inverse.T, noise_ref[...] + forward, ((1,), (0,)))
+
+
+def draw_samples(pieces, noise):
+    return pl.pallas_call(
+        solve_kernel,
+        out_shape=jax.ShapeDtypeStruct((256, 256), F32),
+        scratch_shapes=[
+            pltpu.VMEM((256, 512), F32),
+            pltpu.VMEM((64, 128), F32),
+            pltpu.VMEM((256, 256), F32),
+        ],
+        name="solve",
+    )(pieces, noise)
 
 
 def from_everyone(v, axes, n):
@@ -122,26 +226,8 @@
     part = part.reshape(8, 1, 17 * 128)
     part = jnp.broadcast_to(part, (8, 2, 17 * 128)).reshape(16, 17 * 128)
     part = lax.all_to_all(part, ("z", "yl"), 0, 0, tiled=True).reshape(8, 2 * 17 * 128).sum(0)
-    pieces = from_everyone(part, ("c", "x"), 8).reshape(16, 17, 128)
-
-    packed = jnp.moveaxis(pieces, 0, 1).reshape(272, 128) / 256.0
-    mixed = packed[128:256]
-    first = jnp.tril(mixed, -1) + jnp.diag(packed[256]) + jnp.tril(mixed, -1).T
-    second = jnp.triu(mixed) + jnp.triu(mixed, 1).T
-    corner = packed[0:128]
-    precision = jnp.block([[first, corner.T], [corner, second]])
-    info = packed[257:259].reshape(256, 1)
-    group = lax.axis_index(GROUP)
-    o = lax.dynamic_index_in_dim(order, group, 0, keepdims=False)
-    hi = o >> 4
-    row = (hi & 128) | ((hi & 7) << 4) | ((hi >> 3) & 15)
-    prior = table[:, 128:][row, o & 15]
-    precision = precision + jnp.diag(prior)
-    factor = jnp.linalg.cholesky(precision)
-    forward = lax.linalg.triangular_solve(factor, info, left_side=True, lower=True)
-    return lax.linalg.triangular_solve(
-        factor, forward + noise, left_side=True, lower=True, transpose_a=True
-    )
+    pieces = from_everyone(part, ("c", "x"), 8).reshape(272, 128)
+    return draw_samples(pieces, noise)
 
 
 def solution(mesh):

time: 178 us -> 124 us (0.70)
  other arithmetic: 56.5 us -> 1.26 us
  blocking collectives: 37.2 us -> 59.4 us
  Pallas kernels: 25 us -> 37 us
  waiting for transfers between devices: 22.1 us -> 10.4 us
  starting transfers between devices: 19 us -> 9.58 us
  local copies, waits for them, and re-layouts: 14.1 us -> 5.65 us
    another operation x11 -> x0, other arithmetic: 54.6 us -> none  [the longest x6 33.9 us: per_device(): factor = jnp.linalg.cholesky(precision)]
    pallas_call x0 -> x1, Pallas kernels: none -> 11.9 us  [draw_samples(): pl.pallas_call(solve_kernel, out_shape=jax.ShapeDtypeStruct((256, 256), F...]
    all_to_all x0 -> x1, blocking collectives: none -> 11.3 us  [per_device(): lax.all_to_all(part, ('z', 'yl'), 0, 0, tiled=True).reshape(8, 2 * 17 * 128)]
    all_to_all x1 -> x2, blocking collectives: 17.3 us -> 28.2 us  [from_everyone(): lax.all_to_all(jnp.broadcast_to(v[None], (n, *v.shape)), axes, 0, 0, tile...]
    all_to_all x1 -> x0, waiting for transfers between devices: 8.63 us -> none  [per_device(): lax.all_to_all(part, ('z', 'yl'), 0, 0, tiled=True).reshape(8, 2 * 17 * 128)]
    all_to_all x2 -> x1, starting transfers between devices: 14.7 us -> 8.75 us  [from_everyone(): lax.all_to_all(jnp.broadcast_to(v[None], (n, *v.shape)), axes, 0, 0, tile...]
    another operation x18 -> x0, local copies, waits for them, and re-layouts: 4.37 us -> none
    all_to_all x1 -> x0, starting transfers between devices: 3.51 us -> none  [per_device(): lax.all_to_all(part, ('z', 'yl'), 0, 0, tiled=True).reshape(8, 2 * 17 * 128)]
  transfers between devices with their start and end apart: 4 -> 2, of which waited for: 4 -> 2; matrix products, arithmetic and copies ran while one was open for 2% -> 1% of each run, Pallas kernels for 0% -> 0%
where the time goes in v2:
time: 124 us; the launch traced here: 123 us
  blocking collectives  59.4 us (48%)
  Pallas kernels  37 us (30%)
  waiting for transfers between devices  10.4 us (8%)
  starting transfers between devices  9.58 us (8%)
  local copies, waits for them, and re-layouts  5.65 us (5%)
  other arithmetic  1.26 us (1%)
    all_to_all x2, blocking collectives, from_everyone(): lax.all_to_all(jnp.broadcast_to(v[None], (n, *v.shape)), axes, 0, 0, tile...  28.2 us
    pallas_call x1, Pallas kernels, expert_terms(): pl.pallas_call(expert_kernel, out_shape=(jax.ShapeDtypeStruct((2176, 128)...  25.2 us
    all_to_all x1, blocking collectives, per_device(): lax.all_to_all(own.reshape(16, 136, 128), ('yh', 'x', 'yl'), 0, 0, tiled=...  19.9 us
    pallas_call x1, Pallas kernels, draw_samples(): pl.pallas_call(solve_kernel, out_shape=jax.ShapeDtypeStruct((256, 256), F...  11.9 us
    all_to_all x1, blocking collectives, per_device(): lax.all_to_all(part, ('z', 'yl'), 0, 0, tiled=True).reshape(8, 2 * 17 * 128)  11.3 us
    all_to_all x1, starting transfers between devices, from_everyone(): lax.all_to_all(jnp.broadcast_to(v[None], (n, *v.shape)), axes, 0, 0, tile...  8.75 us
    all_to_all x1, waiting for transfers between devices, from_everyone(): lax.all_to_all(jnp.broadcast_to(v[None], (n, *v.shape)), axes, 0, 0, tile...  7.98 us
    unnamed x7, local copies, waits for them, and re-layouts  3.04 us
  transfers between devices with their start and end apart: 2, of which 2 were waited for; matrix products, arithmetic and copies ran while one was open for 1% of the time, Pallas kernels for 0%

profile of v2, /device:TPU:1, one launch (start us, length us, event | category | flops | bytes accessed | tf_op | source)
XLA Modules:
  0.0 123.4 jit_solution(9831189615183189609)
XLA Ops:
  0.0 0.8 reshape.41
  0.8 0.7 pad_maximum_fusion
  1.4 17.3 %all_to_all.31 = f32[16,1,144]{2,1,0:T(1,128)S(1)} all-to-all(f32[16,1,144]{2,1,0:T(1,128)S(1)} %broadcast_in_dim.15), channel_id=1, replica_groups=mesh['yh'=2,'z'=8,'yl'=2,'x'=4,'c'=2] {'z','yl'}, dimensions={0} | all-to-all | bytes 18432 | tf_op jit(solution)/shard_map/all_to_all | solution.py:214
  18.8 0.7 broadcast_in_dim.33
  19.5 8.8 %all-to-all-start.1 = ((f32[16,16,144]{2,1,0:T(8,128)}), f32[16,16,144]{2,1,0:T(8,128)S(1)}, u32[]{:S(2)}, u32[]{:S(2)}) async-start(f32[16,16,144]{2,1,0:T(8,128)} %broadcast_in_dim.33), calls=%async_computation.1 | async-start | bytes 524288 | tf_op jit(solution)/shard_map/all_to_all | solution.py:214
  28.3 0.7 reshape.40.order_ref
  29.0 8.0 %all-to-all-done.1 = f32[16,16,144]{2,1,0:T(8,128)S(1)} async-done(((f32[16,16,144]{2,1,0:T(8,128)}), f32[16,16,144]{2,1,0:T(8,128)S(1)}, u32[]{:S(2)}, u32[]{:S(2)}) %all-to-all-start.1) | async-done | bytes 147488 | tf_op jit(solution)/shard_map/all_to_all | solution.py:214
  37.0 0.0 copy-start
  37.0 1.6 %copy-done = bf16[1,1024,1024]{2,1,0:T(8,128)(2,1)S(1)} copy-done((bf16[1,1024,1024]{2,1,0:T(8,128)(2,1)S(1)}, bf16[1,1024,1024]{2,1,0:T(8,128)(2,1)}, u32[]{:S(2)}) %copy-start) | copy-done | bytes 2097176
  38.6 0.0 copy-start.1
  38.6 0.8 copy-done.1
  39.3 0.0 copy-start.2
  39.3 0.7 copy-done.2
  40.0 25.2 %expert.1 = (f32[2176,128]{1,0:T(8,128)S(1)}, f32[2176,128]{1,0:T(8,128)S(1)}) custom-call(s32[1]{0:T(128)} %bitcast.me_ref, s32[16,256]{1,0:T(8,128)S(1)} %reshape.40.order_ref, f32[256,144]{1,0:T(8,128)S(1)} %bitcast.7, f32[1,8,1024]{2,1,0:T(8,128)S(1)} %copy-done.1, bf16[1,1024,1024]{2,1,0:T(8,128)(2,1)S(1)} %copy-done, bf16[1,1024]{1,0:T(2,128)(2,1)S(1)} %copy-done.2), custom_call_target="tpu_custom_call" | custom-call | tf_op jit(solution)/shard_map/expert/pallas_call | solution.py:89
  65.2 0.8 collective-permute-start
  66.0 2.4 %collective-permute-done = f32[2176,128]{1,0:T(8,128)S(1)} collective-permute-done((f32[2176,128]{1,0:T(8,128)S(1)}, f32[2176,128]{1,0:T(8,128)S(1)}, u32[]{:S(2)}, u32[]{:S(2)}) %collective-permute-start) | collective-permute-done | bytes 1114144 | tf_op jit(solution)/shard_map/ppermute | solution.py:224
  68.4 0.2 add.3
  68.6 19.9 %all_to_all.32 = f32[16,136,128]{2,1,0:T(8,128)S(1)} all-to-all(f32[16,136,128]{2,1,0:T(8,128)S(1)} %bitcast.8), channel_id=1, replica_groups=mesh['yh'=2,'z'=8,'yl'=2,'x'=4,'c'=2] {'yh','x','yl'}, dimensions={0} | all-to-all | bytes 2228224 | tf_op jit(solution)/shard_map/all_to_all | solution.py:225
  88.4 0.1 reduce_sum.18
  88.6 0.2 all_to_all.23
  88.8 11.3 %all_to_all.33 = f32[16,1,2176]{2,1,0:T(1,128)S(1)} all-to-all(f32[16,1,2176]{2,1,0:T(1,128)S(1)} %all_to_all.23), channel_id=1, replica_groups=mesh['yh'=2,'z'=8,'yl'=2,'x'=4,'c'=2] {'z','yl'}, dimensions={0} | all-to-all | bytes 278528 | tf_op jit(solution)/shard_map/all_to_all | solution.py:228
  100.1 0.3 reduce
  100.5 0.1 broadcast_in_dim.36
  100.6 10.9 %all_to_all.34 = f32[8,1,4352]{2,1,0:T(1,128)} all-to-all(f32[8,1,4352]{2,1,0:T(1,128)S(1)} %broadcast_in_dim.36), channel_id=1, replica_groups=mesh['yh'=2,'z'=8,'yl'=2,'x'=4,'c'=2] {'c','x'}, dimensions={0} | all-to-all | bytes 278528 | tf_op jit(solution)/shard_map/all_to_all | solution.py:214
  111.5 11.9 %solve.1 = f32[256,256]{1,0:T(8,128)} custom-call(f32[272,128]{1,0:T(8,128)} %bitcast.9, f32[256,256]{1,0:T(8,128)} %noise_ref.1), custom_call_target="tpu_custom_call" | custom-call | tf_op jit(solution)/shard_map/solve/pallas_call | solution.py:201
  (6 shorter events, 0.2 us)
Async XLA Ops:
  19.5 17.5 %all-to-all-start.1 = ((f32[16,16,144]{2,1,0:T(8,128)}), f32[16,16,144]{2,1,0:T(8,128)S(1)}, u32[]{:S(2)}, u32[]{:S(2)}) async-start(f32[16,16,144]{2,1,0:T(8,128)} %broadcast_in_dim.33), calls=%async_computation.1 | async-start | bytes 524288 | tf_op jit(solution)/shard_map/all_to_all | solution.py:214
  37.0 1.6 %copy-start = (bf16[1,1024,1024]{2,1,0:T(8,128)(2,1)S(1)}, bf16[1,1024,1024]{2,1,0:T(8,128)(2,1)}, u32[]{:S(2)}) copy-start(bf16[1,1024,1024]{2,1,0:T(8,128)(2,1)} %inv_ref.1) | copy-start | bytes 6291460
  38.6 0.8 copy-start.1
  39.3 0.7 copy-start.2
  65.2 3.2 %collective-permute-start = (f32[2176,128]{1,0:T(8,128)S(1)}, f32[2176,128]{1,0:T(8,128)S(1)}, u32[]{:S(2)}, u32[]{:S(2)}) collective-permute-start(f32[2176,128]{1,0:T(8,128)S(1)} %get-tuple-element.8), channel_id=1, source_target_pairs={{0,1},{1,0},{2,3},{3,2},{4,5},{5,4},{6,7},{7,6},{8,9},{9,8},{10,11... | collective-permute-start | bytes 3342344 | tf_op jit(solution)/shard_map/ppermute | solution.py:224

commit v3 on v2

--- a/solution.py
+++ b/solution.py
@@ -10,6 +10,7 @@
 GROUP = ("yh", "z")
 MEMBER = ("yl", "x", "c")
 RATE = 0.25
+EXPERT_VMEM = 60 << 20
 F32, BF16 = jnp.float32, jnp.bfloat16
 
 
@@ -27,83 +28,135 @@
     return a, b, (v - a - b)
 
 
-def expert_kernel(me_ref, order_ref, table_ref, points_ref, inv_ref, targets_ref,
-                  own_ref, other_ref, parts_s, fold_s, points_s, cross_s):
-    b = pl.program_id(0)
-
-    @pl.when(b == 0)
-    def _():
-        parts_s[0:384, :] = jnp.concatenate(three_parts(table_ref[:, 0:128].T), axis=0).astype(BF16)
-        parts_s[384:432, :] = jnp.concatenate(three_parts(table_ref[:, 128:144].T), axis=0).astype(BF16)
-        fold_s[...] = (iota((32, 432), 1) // 16 == iota((32, 432), 0)).astype(F32).astype(BF16)
-        p = points_ref[0]
-        norm = -RATE * jnp.sum(p * p, axis=0, keepdims=True)
-        h, m, l = three_parts(2.0 * RATE * p)
-        one = jnp.ones((3, p.shape[1]), F32)
-        tail = jnp.concatenate([one, *three_parts(norm), jnp.zeros((2, p.shape[1]), F32)], axis=0)
-        points_s[...] = jnp.concatenate([h, m, l, h, m, l, h, m, l, tail], axis=0).astype(BF16)
-        cross_s[256:272, :] = jnp.where(
-            iota((16, 1024), 0) == 0, jnp.broadcast_to(targets_ref[...].astype(F32), (16, 1024)), 0.0
-        ).astype(BF16)
-
-    o = order_ref[pl.ds(b, 1), :]
-    hi = lax.shift_right_logical(o, 4)
-    row = (hi & 128) | ((hi & 7) << 4) | (lax.shift_right_logical(hi, 3) & 15)
-    hot = jnp.where(iota((256, 256), 0) == row, 1.0, 0.0).astype(BF16)
-    picked = dot(parts_s[...], hot, ((1,), (0,)))
-    picked = jnp.where((iota((432, 256), 0) & 15) == (o & 15), picked, 0.0).astype(BF16)
-    q = dot(fold_s[...], picked, ((1,), (0,)))
-    h, m, l = q[0:8], q[8:16], q[16:24]
-    full = (h + m) + l
-    prior = (q[24:25] + q[25:26]) + q[26:27]
-    norm = -RATE * jnp.sum(full * full, axis=0, keepdims=True)
-    tail = jnp.concatenate([*three_parts(norm), jnp.ones((3, 256), F32), jnp.zeros((2, 256), F32)], axis=0)
-    left = jnp.concatenate([h, h, h, m, m, m, l, l, l, tail], axis=0).T.astype(BF16)
-    power = dot(left, points_s[...], ((1,), (0,)))
-    cross_s[0:256, :] = jnp.exp(power).astype(BF16)
-    proj = dot(cross_s[0:256, :], inv_ref[0], ((1,), (0,))).astype(BF16)
-    terms = dot(cross_s[...], proj, ((1,), (1,)))
-    low = iota((128, 128), 0) - iota((128, 128), 1)
-    first = terms[0:128, 0:128]
-    second = terms[128:256, 128:256] + jnp.where(low == 0, prior[:, 128:256], 0.0)
-    mixed = jnp.where(low > 0, first, second)
-    diag = jnp.sum(jnp.where(low == 0, first, 0.0), axis=0, keepdims=True) + prior[:, 0:128]
-    info = terms[256:257, :]
-    extra = jnp.concatenate([diag, info[:, 0:128], info[:, 128:256], jnp.zeros((13, 128), F32)], axis=0)
+def expert_kernel(me_ref, order_ref, table_ref, points_hbm, inv_hbm, targets_hbm, own_ref, other_ref,
+                  parts_s, fold_s, points_s, cross0_s, cross1_s, proj0_s, proj1_s, left_s, prior_s,
+                  inv_s, raw_s, target_s, sem):
+    copies = [
+        pltpu.make_async_copy(inv_hbm.at[0], inv_s, sem.at[0]),
+        pltpu.make_async_copy(points_hbm.at[0], raw_s, sem.at[1]),
+        pltpu.make_async_copy(targets_hbm, target_s, sem.at[2]),
+    ]
+    for c in copies:
+        c.start()
     core = me_ref[0]
-    start = (b // 8) * 1088 + (b % 8) * 17
-    for r in range(17):
-        if r < 8:
-            rows = terms[128 + 16 * r : 144 + 16 * r, 0:128]
-        elif r < 16:
-            rows = mixed[16 * (r - 8) : 16 * (r - 7), :]
-        else:
-            rows = extra
-        a, c = rows[0:8], rows[8:16]
-        own_ref[pl.ds(start + r, 8, stride=136), :] = jnp.where(core == 0, a, c)
-        other_ref[pl.ds(start + r, 8, stride=136), :] = jnp.where(core == 0, c, a)
+    cross, proj = (cross0_s, cross1_s), (proj0_s, proj1_s)
+
+    def pick(n, carry):
+        o = order_ref[pl.ds(pl.multiple_of(n * 1024, 1024), 1024)].reshape(1, 1024)
+        hi = lax.shift_right_logical(o, 4)
+        row = (hi & 128) | ((hi & 14) << 3) | (lax.shift_right_logical(hi, 3) & 14) | (hi & 1)
+        hot = jnp.where(iota((256, 1024), 0) == row, 1.0, 0.0).astype(BF16)
+        picked = dot(parts_s[...], hot, ((1,), (0,)))
+        picked = jnp.where((iota((432, 1024), 0) & 15) == (o & 15), picked, 0.0).astype(BF16)
+        q = dot(fold_s[...], picked, ((1,), (0,)))
+        h, m, l = q[0:8], q[8:16], q[16:24]
+        full = (h + m) + l
+        norm = -RATE * jnp.sum(full * full, axis=0, keepdims=True)
+        tail = jnp.concatenate([*three_parts(norm), jnp.ones((3, 1024), F32), jnp.zeros((2, 1024), F32)], axis=0)
+        stacked = jnp.concatenate([h, h, h, m, m, m, l, l, l, tail], axis=0)
+        left_s[pl.ds(pl.multiple_of(n * 1024, 1024), 1024), :] = stacked.T.astype(BF16)
+        prior_s[pl.ds(n, 1), :] = (q[24:25] + q[25:26]) + q[26:27]
+        return carry
+
+    def kernel_columns(b, slot, j):
+        at = slice(256 * j, 256 * j + 256)
+        for k in range(2):
+            rows = left_s[pl.ds(pl.multiple_of((b + k) * 256, 256), 256), :]
+            power = dot(rows, points_s[:, at], ((1,), (0,)))
+            cross[slot][272 * k : 272 * k + 256, at] = jnp.exp(power).astype(BF16)
+
+    def write(b, terms, info, prior):
+        low = iota((128, 128), 0) - iota((128, 128), 1)
+        first = terms[0:128, 0:128]
+        second = terms[128:256, 128:256] + jnp.where(low == 0, prior[:, 128:256], 0.0)
+        mixed = jnp.where(low > 0, first, second)
+        diag = jnp.sum(jnp.where(low == 0, first, 0.0), axis=0, keepdims=True) + prior[:, 0:128]
+        extra = jnp.concatenate([diag, info[:, 0:128], info[:, 128:256], jnp.zeros((13, 128), F32)], axis=0)
+        start = (b // 8) * 1088 + (b % 8) * 17
+        for r in range(17):
+            if r < 8:
+                rows = terms[128 + 16 * r : 144 + 16 * r, 0:128]
+            elif r < 16:
+                rows = mixed[16 * (r - 8) : 16 * (r - 7), :]
+            else:
+                rows = extra
+            a, c = rows[0:8], rows[8:16]
+            own_ref[pl.ds(start + r, 8, stride=136), :] = jnp.where(core == 0, a, c)
+            other_ref[pl.ds(start + r, 8, stride=136), :] = jnp.where(core == 0, c, a)
+
+    def precision(b, slot):
+        for k in range(2):
+            terms = dot(
+                cross[slot][256 * k : 256 * k + 272, :], proj[slot][272 * k : 272 * k + 256, :], ((1,), (1,))
+            )
+            prior = prior_s[pl.ds(b // 4, 1), :]
+            at = 512 * slot + 256 * k
+            info = terms[256:257] if k == 0 else terms[0:1]
+            write(b + k, terms[16 * k : 16 * k + 256], info, prior[:, at : at + 256])
+
+    def main(b, slot, before, after):
+        for j in range(4):
+            at = slice(256 * j, 256 * j + 256)
+            proj[slot][:, at] = dot(cross[slot][...], inv_s[:, at], ((1,), (0,))).astype(BF16)
+            if j == 0:
+                precision(before, 1 - slot)
+            kernel_columns(after, 1 - slot, j)
+
+    parts_s[0:384, :] = jnp.concatenate(three_parts(table_ref[:, 0:128].T), axis=0).astype(BF16)
+    parts_s[384:432, :] = jnp.concatenate(three_parts(table_ref[:, 128:144].T), axis=0).astype(BF16)
+    fold_s[...] = (iota((32, 432), 1) // 16 == iota((32, 432), 0)).astype(F32).astype(BF16)
+    lax.fori_loop(0, 4, pick, 0)
+    copies[1].wait()
+    p = raw_s[...]
+    norm = -RATE * jnp.sum(p * p, axis=0, keepdims=True)
+    h, m, l = three_parts(2.0 * RATE * p)
+    one = jnp.ones((3, p.shape[1]), F32)
+    tail = jnp.concatenate([one, *three_parts(norm), jnp.zeros((2, p.shape[1]), F32)], axis=0)
+    points_s[...] = jnp.concatenate([h, m, l, h, m, l, h, m, l, tail], axis=0).astype(BF16)
+    copies[2].wait()
+    goal = jnp.where(
+        iota((16, 1024), 0) == 0, jnp.broadcast_to(target_s[...].astype(F32), (16, 1024)), 0.0
+    ).astype(BF16)
+    cross0_s[256:272, :] = goal
+    cross1_s[256:272, :] = goal
+    for j in range(4):
+        kernel_columns(0, 0, j)
+    copies[0].wait()
+
+    def step(i, carry):
+        b = 4 * i
+        main(b, 0, jnp.maximum(b - 2, 0), b + 2)
+        main(b + 2, 1, b, jnp.minimum(b + 4, 14))
+        return carry
+
+    lax.fori_loop(0, 4, step, 0)
+    precision(14, 1)
 
 
 def expert_terms(core, order, table, points, inverse_cov, targets):
-    whole = lambda *shape: pl.BlockSpec(shape, lambda b, me: (0,) * len(shape))
+    vmem = pl.BlockSpec(memory_space=pltpu.VMEM)
+    hbm = pl.BlockSpec(memory_space=pltpu.HBM)
     return pl.pallas_call(
         expert_kernel,
         out_shape=(jax.ShapeDtypeStruct((2176, 128), F32),) * 2,
-        grid_spec=pltpu.PrefetchScalarGridSpec(
-            num_scalar_prefetch=1,
-            grid=(16,),
-            in_specs=[whole(16, 256), whole(256, 144), whole(1, 8, 1024), whole(1, 1024, 1024), whole(1, 1024)],
-            out_specs=(whole(2176, 128),) * 2,
-            scratch_shapes=[
-                pltpu.VMEM((432, 256), BF16),
-                pltpu.VMEM((32, 432), BF16),
-                pltpu.VMEM((80, 1024), BF16),
-                pltpu.VMEM((272, 1024), BF16),
-            ],
-        ),
-        compiler_params=pltpu.CompilerParams(
-            dimension_semantics=("arbitrary",), vmem_limit_bytes=40 << 20
-        ),
+        in_specs=[pl.BlockSpec(memory_space=pltpu.SMEM), vmem, vmem, hbm, hbm, hbm],
+        out_specs=(vmem, vmem),
+        scratch_shapes=[
+            pltpu.VMEM((432, 256), BF16),
+            pltpu.VMEM((32, 432), BF16),
+            pltpu.VMEM((80, 1024), BF16),
+            pltpu.VMEM((528, 1024), BF16),
+            pltpu.VMEM((528, 1024), BF16),
+            pltpu.VMEM((528, 1024), BF16),
+            pltpu.VMEM((528, 1024), BF16),
+            pltpu.VMEM((4096, 80), BF16),
+            pltpu.VMEM((8, 1024), F32),
+            pltpu.VMEM((1024, 1024), BF16),
+            pltpu.VMEM((8, 1024), F32),
+            pltpu.VMEM((1, 1024), BF16),
+            pltpu.SemaphoreType.DMA((3,)),
+        ],
+        compiler_params=pltpu.CompilerParams(vmem_limit_bytes=EXPERT_VMEM),
         name="expert",
     )(core, order, table, points, inverse_cov, targets)
 
@@ -152,8 +205,9 @@
     scale = 1.0 / 256.0
 
     def packed(r):
+        at = slice(128 * r, 128 * r + 128)
         return jnp.concatenate(
-            [pieces_ref[pl.ds(r, 8, stride=17), :], pieces_ref[pl.ds(136 + r, 8, stride=17), :]], axis=0
+            [pieces_ref[v, :, at] for v in range(8)], axis=0
         ) * scale
 
     corner = jnp.concatenate([packed(r) for r in range(8)], axis=0)
@@ -216,17 +270,17 @@
 
 def per_device(points, inverse_cov, targets, queries, prior_precision, batch_order, noise):
     mine = jnp.concatenate([queries.reshape(-1), prior_precision])
-    table = from_everyone(mine, ("z", "yl"), 16)
-    table = from_everyone(table, ("yh", "x", "c"), 16).reshape(256, 144)
-    order = batch_order.reshape(16, 256)
-    core = lax.axis_index("c")
-    own, other = expert_terms(core[None], order, table, points, inverse_cov, targets)
+    core = lax.axis_index("c")[None]
+    mine, core = lax.optimization_barrier((mine, core))
+    table = from_everyone(mine, ("z", "c"), 16)
+    table = from_everyone(table, ("yh", "yl", "x"), 16).reshape(256, 144)
+    own, other = expert_terms(core, batch_order, table, points, inverse_cov, targets)
     own = own + lax.ppermute(other, "c", [(0, 1), (1, 0)])
-    part = lax.all_to_all(own.reshape(16, 136, 128), ("yh", "x", "yl"), 0, 0, tiled=True).sum(0)
-    part = part.reshape(8, 1, 17 * 128)
-    part = jnp.broadcast_to(part, (8, 2, 17 * 128)).reshape(16, 17 * 128)
-    part = lax.all_to_all(part, ("z", "yl"), 0, 0, tiled=True).reshape(8, 2 * 17 * 128).sum(0)
-    pieces = from_everyone(part, ("c", "x"), 8).reshape(272, 128)
+    part = lax.all_to_all(own.reshape(8, 272, 128), ("yh", "x"), 0, 0, tiled=True).sum(0)
+    part = jnp.swapaxes(part.reshape(2, 8, 2176), 0, 1)
+    part = jnp.broadcast_to(part[None], (2, 8, 2, 2176)).reshape(16, 2, 2176)
+    part = lax.all_to_all(part, ("yl", "z"), 0, 0, tiled=True).sum(0)
+    pieces = from_everyone(part, ("c", "x"), 8)
     return draw_samples(pieces, noise)
 
 

time: 124 us -> 115 us (0.927)
  blocking collectives: 59.4 us -> 74.5 us
  starting transfers between devices: 9.58 us -> 1.61 us
  waiting for transfers between devices: 10.4 us -> 2.59 us
  Pallas kernels: 37 us -> 32.2 us
  local copies, waits for them, and re-layouts: 5.65 us -> 1.01 us
    all_to_all x2 -> x3, blocking collectives: 28.2 us -> 42.7 us  [from_everyone(): lax.all_to_all(jnp.broadcast_to(v[None], (n, *v.shape)), axes, 0, 0, tile...]
    all_to_all x1 -> x0, starting transfers between devices: 8.75 us -> none  [from_everyone(): lax.all_to_all(jnp.broadcast_to(v[None], (n, *v.shape)), axes, 0, 0, tile...]
    all_to_all x1 -> x0, waiting for transfers between devices: 7.98 us -> none  [from_everyone(): lax.all_to_all(jnp.broadcast_to(v[None], (n, *v.shape)), axes, 0, 0, tile...]
    pallas_call x1, Pallas kernels: 25.2 us -> 20.3 us  [expert_terms(): pl.pallas_call(expert_kernel, out_shape=(jax.ShapeDtypeStruct((2176, 128)...]
    unnamed x7 -> x1, local copies, waits for them, and re-layouts: 3.04 us -> 0.01 us
  transfers between devices with their start and end apart: 2 -> 1, of which waited for: 2 -> 1; matrix products, arithmetic and copies ran while one was open for 1% -> 0% of each run, Pallas kernels for 0% -> 0%
where the time goes in v3:
time: 115 us; the launch traced here: 114 us
  blocking collectives  74.5 us (65%)
  Pallas kernels  32.2 us (28%)
  waiting for transfers between devices  2.59 us (2%)
  other arithmetic  2.18 us (2%)
  starting transfers between devices  1.61 us (1%)
    all_to_all x3, blocking collectives, from_everyone(): lax.all_to_all(jnp.broadcast_to(v[None], (n, *v.shape)), axes, 0, 0, tile...  42.7 us
    all_to_all x1, blocking collectives, per_device(): lax.all_to_all(own.reshape(8, 272, 128), ('yh', 'x'), 0, 0, tiled=True)  20.4 us
    pallas_call x1, Pallas kernels, expert_terms(): pl.pallas_call(expert_kernel, out_shape=(jax.ShapeDtypeStruct((2176, 128)...  20.3 us
    pallas_call x1, Pallas kernels, draw_samples(): pl.pallas_call(solve_kernel, out_shape=jax.ShapeDtypeStruct((256, 256), F...  11.9 us
    all_to_all x1, blocking collectives, per_device(): part = lax.all_to_all(part, ('yl', 'z'), 0, 0, tiled=True).sum(0)  11.5 us
    ppermute x1, waiting for transfers between devices, per_device(): own = own + lax.ppermute(other, 'c', [(0, 1), (1, 0)])  2.59 us
  transfers between devices with their start and end apart: 1, of which 1 were waited for; matrix products, arithmetic and copies ran while one was open for 0% of the time, Pallas kernels for 0%

profile of v3, /device:TPU:1, one launch (start us, length us, event | category | flops | bytes accessed | tf_op | source)
XLA Modules:
  0.0 114.2 jit_solution(13837609601714205062)
XLA Ops:
  0.0 0.8 reshape.25
  0.8 0.7 pad_maximum_fusion
  1.4 17.1 %all_to_all.26 = f32[16,1,144]{2,1,0:T(1,128)S(1)} all-to-all(f32[16,1,144]{2,1,0:T(1,128)S(1)} %broadcast_in_dim.13), channel_id=1, replica_groups=mesh['yh'=2,'z'=8,'yl'=2,'x'=4,'c'=2] {'z','c'}, dimensions={0} | all-to-all | bytes 18432 | tf_op jit(solution)/shard_map/all_to_all | solution.py:268
  18.6 14.8 %all_to_all.27 = f32[16,16,144]{2,1,0:T(8,128)} all-to-all(f32[16,16,144]{2,1,0:T(8,128)S(1)} %broadcast_in_dim.15), channel_id=1, replica_groups=mesh['yh'=2,'z'=8,'yl'=2,'x'=4,'c'=2] {'yh','yl','x'}, dimensions={0} | all-to-all | bytes 294912 | tf_op jit(solution)/shard_map/all_to_all | solution.py:268
  33.3 20.3 %expert.1 = (f32[2176,128]{1,0:T(8,128)}, f32[2176,128]{1,0:T(8,128)}) custom-call(s32[1]{0:T(128)} %bitcast.me_ref, s32[4096]{0:T(1024)} %order_ref.1, f32[256,144]{1,0:T(8,128)} %bitcast.10, f32[1,8,1024]{2,1,0:T(8,128)} %points_hbm.1, bf16[1,1024,1024]{2,1,0:T(8,128)(2,1)} %inv_hbm.1, bf16[1,1024]{1,0:T(2,128)(2,1)} %targets_hbm.1), custom_call_target="tpu_custom_call" | custom-call | tf_op jit(solution)/shard_map/expert/pallas_call | solution.py:139
  53.7 1.6 %collective-permute-start = (f32[2176,128]{1,0:T(8,128)}, f32[2176,128]{1,0:T(8,128)S(1)}, u32[]{:S(2)}, u32[]{:S(2)}) collective-permute-start(f32[2176,128]{1,0:T(8,128)} %get-tuple-element.12), channel_id=1, source_target_pairs={{0,1},{1,0},{2,3},{3,2},{4,5},{5,4},{6,7},{7,6},{8,9},{9,8},{10,11... | collective-permute-start | bytes 3342344 | tf_op jit(solution)/shard_map/ppermute | solution.py:278
  55.3 2.6 %collective-permute-done = f32[2176,128]{1,0:T(8,128)S(1)} collective-permute-done((f32[2176,128]{1,0:T(8,128)}, f32[2176,128]{1,0:T(8,128)S(1)}, u32[]{:S(2)}, u32[]{:S(2)}) %collective-permute-start) | collective-permute-done | bytes 1114144 | tf_op jit(solution)/shard_map/ppermute | solution.py:278
  57.9 1.4 %add.3 = f32[2176,128]{1,0:T(8,128)S(1)} add(f32[2176,128]{1,0:T(8,128)} %get-tuple-element.11, f32[2176,128]{1,0:T(8,128)S(1)} %collective-permute-done) | non-fusion elementwise | flops 278528 | bytes 3342336 | tf_op jit(solution)/shard_map/add | solution.py:278
  59.2 20.4 %all_to_all.28 = f32[8,272,128]{2,1,0:T(8,128)S(1)} all-to-all(f32[8,272,128]{2,1,0:T(8,128)S(1)} %bitcast.8), channel_id=1, replica_groups=mesh['yh'=2,'z'=8,'yl'=2,'x'=4,'c'=2] {'yh','x'}, dimensions={0} | all-to-all | bytes 2228224 | tf_op jit(solution)/shard_map/all_to_all | solution.py:279
  79.6 0.1 reduce_sum.18
  79.7 0.1 copy.11
  79.8 0.1 broadcast_in_dim.16
  79.9 11.5 %all_to_all.29 = f32[16,2,2176]{2,1,0:T(2,128)S(1)} all-to-all(f32[16,2,2176]{2,1,0:T(2,128)S(1)} %bitcast.9), channel_id=1, replica_groups=mesh['yh'=2,'z'=8,'yl'=2,'x'=4,'c'=2] {'yl','z'}, dimensions={0} | all-to-all | bytes 557056 | tf_op jit(solution)/shard_map/all_to_all | solution.py:282
  91.3 0.1 reduce_sum.19
  91.5 10.8 %all_to_all.30.pieces_ref = f32[8,2,2176]{2,1,0:T(2,128)} all-to-all(f32[8,2,2176]{2,1,0:T(2,128)S(1)} %broadcast_in_dim.34), channel_id=1, replica_groups=mesh['yh'=2,'z'=8,'yl'=2,'x'=4,'c'=2] {'c','x'}, dimensions={0} | all-to-all | bytes 278528 | tf_op jit(solution)/shard_map/all_to_all | solution.py:268
  102.3 11.9 %solve.1 = f32[256,256]{1,0:T(8,128)} custom-call(f32[8,2,2176]{2,1,0:T(2,128)} %all_to_all.30.pieces_ref, f32[256,256]{1,0:T(8,128)} %noise_ref.1), custom_call_target="tpu_custom_call" | custom-call | tf_op jit(solution)/shard_map/solve/pallas_call | solution.py:255
  (5 shorter events, 0.1 us)
Async XLA Ops:
  53.7 4.2 %collective-permute-start = (f32[2176,128]{1,0:T(8,128)}, f32[2176,128]{1,0:T(8,128)S(1)}, u32[]{:S(2)}, u32[]{:S(2)}) collective-permute-start(f32[2176,128]{1,0:T(8,128)} %get-tuple-element.12), channel_id=1, source_target_pairs={{0,1},{1,0},{2,3},{3,2},{4,5},{5,4},{6,7},{7,6},{8,9},{9,8},{10,11... | collective-permute-start | bytes 3342344 | tf_op jit(solution)/shard_map/ppermute | solution.py:278

commit v4 on v3

--- a/solution.py
+++ b/solution.py
@@ -178,9 +178,8 @@
 def factor_block(groups, done_ref):
     for p in range(8):
         g = groups[p]
-        cols = [along_lanes(g, 8 * p + j) for j in range(8)]
-        b = [[along_rows(cols[j], i) for j in range(i + 1)] for i in range(8)]
         rows = [along_rows(g, i) for i in range(8)]
+        b = [[along_lanes(rows[i], 8 * p + j) for j in range(i + 1)] for i in range(8)]
         ahead = [[along_lanes(groups[t], 8 * p + j) for j in range(8)] for t in range(p + 1, 8)]
         for k in range(8):
             r = lax.rsqrt(b[k][k])
@@ -202,13 +201,11 @@
 
 
 def solve_kernel(pieces_ref, noise_ref, out_ref, aug_s, done_s, inverse_s):
-    scale = 1.0 / 256.0
-
     def packed(r):
         at = slice(128 * r, 128 * r + 128)
         return jnp.concatenate(
             [pieces_ref[v, :, at] for v in range(8)], axis=0
-        ) * scale
+        )
 
     corner = jnp.concatenate([packed(r) for r in range(8)], axis=0)
     mixed = jnp.concatenate([packed(r) for r in range(8, 16)], axis=0)
@@ -269,13 +266,15 @@
 
 
 def per_device(points, inverse_cov, targets, queries, prior_precision, batch_order, noise):
-    mine = jnp.concatenate([queries.reshape(-1), prior_precision])
+    mine = lax.optimization_barrier(jnp.concatenate([queries, prior_precision[None]], axis=0)).reshape(-1)
     core = lax.axis_index("c")[None]
     mine, core = lax.optimization_barrier((mine, core))
     table = from_everyone(mine, ("z", "c"), 16)
     table = from_everyone(table, ("yh", "yl", "x"), 16).reshape(256, 144)
     own, other = expert_terms(core, batch_order, table, points, inverse_cov, targets)
-    own = own + lax.ppermute(other, "c", [(0, 1), (1, 0)])
+    scale = 1.0 / 256.0
+    theirs = lax.ppermute(other, "c", [(0, 1), (1, 0)])
+    own = lax.optimization_barrier(own * scale) + theirs * scale
     part = lax.all_to_all(own.reshape(8, 272, 128), ("yh", "x"), 0, 0, tiled=True).sum(0)
     part = jnp.swapaxes(part.reshape(2, 8, 2176), 0, 1)
     part = jnp.broadcast_to(part[None], (2, 8, 2, 2176)).reshape(16, 2, 2176)

time: 115 us -> 113 us (0.983)
  waiting for transfers between devices: 2.59 us -> 1.27 us
    ppermute x1, waiting for transfers between devices: 2.59 us -> 1.27 us  [per_device(): theirs = lax.ppermute(other, 'c', [(0, 1), (1, 0)])]
    mul x0 -> x1, other arithmetic: none -> 1.32 us  [per_device(): own = lax.optimization_barrier(own * scale) + theirs * scale]
    add x1, other arithmetic: 1.36 us -> 0.11 us  [per_device(): own = lax.optimization_barrier(own * scale) + theirs * scale]
  transfers between devices with their start and end apart: 1 -> 1, of which waited for: 1 -> 1; matrix products, arithmetic and copies ran while one was open for 0% -> 1% of each run, Pallas kernels for 0% -> 0%
where the time goes in v4:
time: 113 us; the launch traced here: 112 us
  blocking collectives  74.5 us (66%)
  Pallas kernels  32.2 us (28%)
  other arithmetic  2.29 us (2%)
  starting transfers between devices  1.63 us (1%)
  waiting for transfers between devices  1.27 us (1%)
    all_to_all x3, blocking collectives, from_everyone(): lax.all_to_all(jnp.broadcast_to(v[None], (n, *v.shape)), axes, 0, 0, tile...  42.7 us
    all_to_all x1, blocking collectives, per_device(): lax.all_to_all(own.reshape(8, 272, 128), ('yh', 'x'), 0, 0, tiled=True)  20.4 us
    pallas_call x1, Pallas kernels, expert_terms(): pl.pallas_call(expert_kernel, out_shape=(jax.ShapeDtypeStruct((2176, 128)...  20.3 us
    pallas_call x1, Pallas kernels, draw_samples(): pl.pallas_call(solve_kernel, out_shape=jax.ShapeDtypeStruct((256, 256), F...  11.9 us
    all_to_all x1, blocking collectives, per_device(): part = lax.all_to_all(part, ('yl', 'z'), 0, 0, tiled=True).sum(0)  11.5 us
  transfers between devices with their start and end apart: 1, of which 1 were waited for; matrix products, arithmetic and copies ran while one was open for 1% of the time, Pallas kernels for 0%

profile of v4, /device:TPU:1, one launch (start us, length us, event | category | flops | bytes accessed | tf_op | source)
XLA Modules:
  0.0 112.3 jit_solution(17586796378985449751)
XLA Ops:
  0.0 0.7 pad_maximum_fusion
  0.7 0.1 reshape.25
  0.8 17.1 %all_to_all.26 = f32[16,1,144]{2,1,0:T(1,128)S(1)} all-to-all(f32[16,1,144]{2,1,0:T(1,128)S(1)} %broadcast_in_dim.16), channel_id=1, replica_groups=mesh['yh'=2,'z'=8,'yl'=2,'x'=4,'c'=2] {'z','c'}, dimensions={0} | all-to-all | bytes 18432 | tf_op jit(solution)/shard_map/all_to_all | solution.py:265
  17.9 14.8 %all_to_all.27 = f32[16,16,144]{2,1,0:T(8,128)} all-to-all(f32[16,16,144]{2,1,0:T(8,128)S(1)} %broadcast_in_dim.36), channel_id=1, replica_groups=mesh['yh'=2,'z'=8,'yl'=2,'x'=4,'c'=2] {'yh','yl','x'}, dimensions={0} | all-to-all | bytes 294912 | tf_op jit(solution)/shard_map/all_to_all | solution.py:265
  32.7 20.3 %expert.1 = (f32[2176,128]{1,0:T(8,128)}, f32[2176,128]{1,0:T(8,128)}) custom-call(s32[1]{0:T(128)} %bitcast.1.me_ref, s32[4096]{0:T(1024)} %order_ref.1, f32[256,144]{1,0:T(8,128)} %bitcast.11, f32[1,8,1024]{2,1,0:T(8,128)} %points_hbm.1, bf16[1,1024,1024]{2,1,0:T(8,128)(2,1)} %inv_hbm.1, bf16[1,1024]{1,0:T(2,128)(2,1)} %targets_hbm.1), custom_call_target="tpu_custom_call" | custom-call | tf_op jit(solution)/shard_map/expert/pallas_call | solution.py:139
  53.0 1.6 %collective-permute-start = (f32[2176,128]{1,0:T(8,128)}, f32[2176,128]{1,0:T(8,128)S(1)}, u32[]{:S(2)}, u32[]{:S(2)}) collective-permute-start(f32[2176,128]{1,0:T(8,128)} %get-tuple-element.12), channel_id=1, source_target_pairs={{0,1},{1,0},{2,3},{3,2},{4,5},{5,4},{6,7},{7,6},{8,9},{9,8},{10,11... | collective-permute-start | bytes 3342344 | tf_op jit(solution)/shard_map/ppermute | solution.py:276
  54.7 1.3 %broadcast_multiply_fusion = f32[2176,128]{1,0:T(8,128)S(1)} fusion(f32[2176,128]{1,0:T(8,128)} %get-tuple-element.11), kind=kLoop, calls=%fused_computation.1 | loop fusion | flops 278528 | bytes 2228224 | tf_op jit(solution)/shard_map/mul | solution.py:277
  56.0 1.3 %collective-permute-done = f32[2176,128]{1,0:T(8,128)S(1)} collective-permute-done((f32[2176,128]{1,0:T(8,128)}, f32[2176,128]{1,0:T(8,128)S(1)}, u32[]{:S(2)}, u32[]{:S(2)}) %collective-permute-start) | collective-permute-done | bytes 1114144 | tf_op jit(solution)/shard_map/ppermute | solution.py:276
  57.2 0.1 multiply_add_fusion
  57.4 20.4 %all_to_all.28 = f32[8,272,128]{2,1,0:T(8,128)S(1)} all-to-all(f32[8,272,128]{2,1,0:T(8,128)S(1)} %bitcast.9), channel_id=1, replica_groups=mesh['yh'=2,'z'=8,'yl'=2,'x'=4,'c'=2] {'yh','x'}, dimensions={0} | all-to-all | bytes 2228224 | tf_op jit(solution)/shard_map/all_to_all | solution.py:278
  77.7 0.1 reduce_sum.18
  77.8 0.1 copy.11
  77.9 0.1 broadcast_in_dim.37
  78.0 11.5 %all_to_all.29 = f32[16,2,2176]{2,1,0:T(2,128)S(1)} all-to-all(f32[16,2,2176]{2,1,0:T(2,128)S(1)} %bitcast.10), channel_id=1, replica_groups=mesh['yh'=2,'z'=8,'yl'=2,'x'=4,'c'=2] {'yl','z'}, dimensions={0} | all-to-all | bytes 557056 | tf_op jit(solution)/shard_map/all_to_all | solution.py:281
  89.5 0.1 reduce_sum.19
  89.6 10.8 %all_to_all.30.pieces_ref = f32[8,2,2176]{2,1,0:T(2,128)} all-to-all(f32[8,2,2176]{2,1,0:T(2,128)S(1)} %broadcast_in_dim.38), channel_id=1, replica_groups=mesh['yh'=2,'z'=8,'yl'=2,'x'=4,'c'=2] {'c','x'}, dimensions={0} | all-to-all | bytes 278528 | tf_op jit(solution)/shard_map/all_to_all | solution.py:265
  100.4 11.9 %solve.1 = f32[256,256]{1,0:T(8,128)} custom-call(f32[8,2,2176]{2,1,0:T(2,128)} %all_to_all.30.pieces_ref, f32[256,256]{1,0:T(8,128)} %noise_ref.1), custom_call_target="tpu_custom_call" | custom-call | tf_op jit(solution)/shard_map/solve/pallas_call | solution.py:252
  (5 shorter events, 0.1 us)
Async XLA Ops:
  53.0 4.2 %collective-permute-start = (f32[2176,128]{1,0:T(8,128)}, f32[2176,128]{1,0:T(8,128)S(1)}, u32[]{:S(2)}, u32[]{:S(2)}) collective-permute-start(f32[2176,128]{1,0:T(8,128)} %get-tuple-element.12), channel_id=1, source_target_pairs={{0,1},{1,0},{2,3},{3,2},{4,5},{5,4},{6,7},{7,6},{8,9},{9,8},{10,11... | collective-permute-start | bytes 3342344 | tf_op jit(solution)/shard_map/ppermute | solution.py:276

commit v5 on v4

--- a/solution.py
+++ b/solution.py
@@ -171,15 +171,15 @@
     return jnp.broadcast_to(v[:, i : i + 1], (8, 128))
 
 
-def along_rows(v, i):
-    return jnp.broadcast_to(v[i : i + 1, :], (8, 128))
-
-
-def factor_block(groups, done_ref):
+def factor_block(groups, done_ref, splat_ref):
     for p in range(8):
         g = groups[p]
-        rows = [along_rows(g, i) for i in range(8)]
-        b = [[along_lanes(rows[i], 8 * p + j) for j in range(i + 1)] for i in range(8)]
+        at = 72 * p
+        for j in range(8):
+            splat_ref[at + 8 * j : at + 8 * j + 8, :] = along_lanes(g, 8 * p + j)
+        splat_ref[at + 64 : at + 72, :] = g
+        b = [[splat_ref[pl.ds(at + 8 * j + i, 8, stride=0), :] for j in range(i + 1)] for i in range(8)]
+        rows = [splat_ref[pl.ds(at + 64 + i, 8, stride=0), :] for i in range(8)]
         ahead = [[along_lanes(groups[t], 8 * p + j) for j in range(8)] for t in range(p + 1, 8)]
         for k in range(8):
             r = lax.rsqrt(b[k][k])
@@ -200,7 +200,7 @@
             done_ref[8 * p + k : 8 * p + k + 1, :] = rows[k][0:1]
 
 
-def solve_kernel(pieces_ref, noise_ref, out_ref, aug_s, done_s, inverse_s):
+def solve_kernel(pieces_ref, noise_ref, out_ref, aug_s, done_s, inverse_s, splat_s):
     def packed(r):
         at = slice(128 * r, 128 * r + 128)
         return jnp.concatenate(
@@ -228,7 +228,7 @@
         if s % 2:
             block = pltpu.roll(block, 64, 1)
         block = jnp.where(lane < 64, block, unit)
-        factor_block([block[8 * t : 8 * t + 8] for t in range(8)], done_s)
+        factor_block([block[8 * t : 8 * t + 8] for t in range(8)], done_s, splat_s)
         inv = pltpu.roll(done_s[...], 64, 1)[:, 0:64]
         wide = 128 * (s // 2 + 1)
         inverse = exact_dot(inv, aug_s[top : top + 64, 256 : 256 + wide], ((1,), (0,)))
@@ -256,6 +256,7 @@
             pltpu.VMEM((256, 512), F32),
             pltpu.VMEM((64, 128), F32),
             pltpu.VMEM((256, 256), F32),
+            pltpu.VMEM((584, 128), F32),
         ],
         name="solve",
     )(pieces, noise)

time: 113 us -> 111 us (0.982)
  Pallas kernels: 32.2 us -> 30.7 us
    pallas_call x1, Pallas kernels: 11.9 us -> 10.4 us  [draw_samples(): pl.pallas_call(solve_kernel, out_shape=jax.ShapeDtypeStruct((256, 256), F...]
where the time goes in v5:
time: 111 us
  blocking collectives  74.5 us (67%)
  Pallas kernels  30.7 us (28%)
  other arithmetic  2.29 us (2%)
  starting transfers between devices  1.63 us (1%)
  waiting for transfers between devices  1.27 us (1%)
    all_to_all x3, blocking collectives, from_everyone(): lax.all_to_all(jnp.broadcast_to(v[None], (n, *v.shape)), axes, 0, 0, tile...  42.7 us
    all_to_all x1, blocking collectives, per_device(): lax.all_to_all(own.reshape(8, 272, 128), ('yh', 'x'), 0, 0, tiled=True)  20.4 us
    pallas_call x1, Pallas kernels, expert_terms(): pl.pallas_call(expert_kernel, out_shape=(jax.ShapeDtypeStruct((2176, 128)...  20.3 us
    all_to_all x1, blocking collectives, per_device(): part = lax.all_to_all(part, ('yl', 'z'), 0, 0, tiled=True).sum(0)  11.5 us
    pallas_call x1, Pallas kernels, draw_samples(): pl.pallas_call(solve_kernel, out_shape=jax.ShapeDtypeStruct((256, 256), F...  10.4 us
  transfers between devices with their start and end apart: 1, of which 1 were waited for; matrix products, arithmetic and copies ran while one was open for 1% of the time, Pallas kernels for 0%

profile of v5, /device:TPU:1, one launch (start us, length us, event | category | flops | bytes accessed | tf_op | source)
XLA Modules:
  0.0 110.8 jit_solution(11396832031409043400)
XLA Ops:
  0.0 0.7 pad_maximum_fusion
  0.7 0.1 reshape.25
  0.8 17.1 %all_to_all.26 = f32[16,1,144]{2,1,0:T(1,128)S(1)} all-to-all(f32[16,1,144]{2,1,0:T(1,128)S(1)} %broadcast_in_dim.16), channel_id=1, replica_groups=mesh['yh'=2,'z'=8,'yl'=2,'x'=4,'c'=2] {'z','c'}, dimensions={0} | all-to-all | bytes 18432 | tf_op jit(solution)/shard_map/all_to_all | solution.py:266
  17.9 14.8 %all_to_all.27 = f32[16,16,144]{2,1,0:T(8,128)} all-to-all(f32[16,16,144]{2,1,0:T(8,128)S(1)} %broadcast_in_dim.36), channel_id=1, replica_groups=mesh['yh'=2,'z'=8,'yl'=2,'x'=4,'c'=2] {'yh','yl','x'}, dimensions={0} | all-to-all | bytes 294912 | tf_op jit(solution)/shard_map/all_to_all | solution.py:266
  32.7 20.3 %expert.1 = (f32[2176,128]{1,0:T(8,128)}, f32[2176,128]{1,0:T(8,128)}) custom-call(s32[1]{0:T(128)} %bitcast.1.me_ref, s32[4096]{0:T(1024)} %order_ref.1, f32[256,144]{1,0:T(8,128)} %bitcast.11, f32[1,8,1024]{2,1,0:T(8,128)} %points_hbm.1, bf16[1,1024,1024]{2,1,0:T(8,128)(2,1)} %inv_hbm.1, bf16[1,1024]{1,0:T(2,128)(2,1)} %targets_hbm.1), custom_call_target="tpu_custom_call" | custom-call | tf_op jit(solution)/shard_map/expert/pallas_call | solution.py:139
  53.0 1.6 %collective-permute-start = (f32[2176,128]{1,0:T(8,128)}, f32[2176,128]{1,0:T(8,128)S(1)}, u32[]{:S(2)}, u32[]{:S(2)}) collective-permute-start(f32[2176,128]{1,0:T(8,128)} %get-tuple-element.12), channel_id=1, source_target_pairs={{0,1},{1,0},{2,3},{3,2},{4,5},{5,4},{6,7},{7,6},{8,9},{9,8},{10,11... | collective-permute-start | bytes 3342344 | tf_op jit(solution)/shard_map/ppermute | solution.py:277
  54.7 1.3 %broadcast_multiply_fusion = f32[2176,128]{1,0:T(8,128)S(1)} fusion(f32[2176,128]{1,0:T(8,128)} %get-tuple-element.11), kind=kLoop, calls=%fused_computation.1 | loop fusion | flops 278528 | bytes 2228224 | tf_op jit(solution)/shard_map/mul | solution.py:278
  56.0 1.3 %collective-permute-done = f32[2176,128]{1,0:T(8,128)S(1)} collective-permute-done((f32[2176,128]{1,0:T(8,128)}, f32[2176,128]{1,0:T(8,128)S(1)}, u32[]{:S(2)}, u32[]{:S(2)}) %collective-permute-start) | collective-permute-done | bytes 1114144 | tf_op jit(solution)/shard_map/ppermute | solution.py:277
  57.2 0.1 multiply_add_fusion
  57.4 20.4 %all_to_all.28 = f32[8,272,128]{2,1,0:T(8,128)S(1)} all-to-all(f32[8,272,128]{2,1,0:T(8,128)S(1)} %bitcast.9), channel_id=1, replica_groups=mesh['yh'=2,'z'=8,'yl'=2,'x'=4,'c'=2] {'yh','x'}, dimensions={0} | all-to-all | bytes 2228224 | tf_op jit(solution)/shard_map/all_to_all | solution.py:279
  77.7 0.1 reduce_sum.18
  77.8 0.1 copy.11
  77.9 0.1 broadcast_in_dim.37
  78.0 11.5 %all_to_all.29 = f32[16,2,2176]{2,1,0:T(2,128)S(1)} all-to-all(f32[16,2,2176]{2,1,0:T(2,128)S(1)} %bitcast.10), channel_id=1, replica_groups=mesh['yh'=2,'z'=8,'yl'=2,'x'=4,'c'=2] {'yl','z'}, dimensions={0} | all-to-all | bytes 557056 | tf_op jit(solution)/shard_map/all_to_all | solution.py:282
  89.5 0.1 reduce_sum.19
  89.6 10.8 %all_to_all.30.pieces_ref = f32[8,2,2176]{2,1,0:T(2,128)} all-to-all(f32[8,2,2176]{2,1,0:T(2,128)S(1)} %broadcast_in_dim.38), channel_id=1, replica_groups=mesh['yh'=2,'z'=8,'yl'=2,'x'=4,'c'=2] {'c','x'}, dimensions={0} | all-to-all | bytes 278528 | tf_op jit(solution)/shard_map/all_to_all | solution.py:266
  100.4 10.4 %solve.1 = f32[256,256]{1,0:T(8,128)} custom-call(f32[8,2,2176]{2,1,0:T(2,128)} %all_to_all.30.pieces_ref, f32[256,256]{1,0:T(8,128)} %noise_ref.1), custom_call_target="tpu_custom_call" | custom-call | tf_op jit(solution)/shard_map/solve/pallas_call | solution.py:252
  (5 shorter events, 0.1 us)
Async XLA Ops:
  53.0 4.2 %collective-permute-start = (f32[2176,128]{1,0:T(8,128)}, f32[2176,128]{1,0:T(8,128)S(1)}, u32[]{:S(2)}, u32[]{:S(2)}) collective-permute-start(f32[2176,128]{1,0:T(8,128)} %get-tuple-element.12), channel_id=1, source_target_pairs={{0,1},{1,0},{2,3},{3,2},{4,5},{5,4},{6,7},{7,6},{8,9},{9,8},{10,11... | collective-permute-start | bytes 3342344 | tf_op jit(solution)/shard_map/ppermute | solution.py:277
